TPU v7x, 256 devices: a whole 4x4x8 slice. The times are simulated.
256 devices in a mesh: ma: 64 (over y, z, core), vert: 4 (over x).
Axes of the slice: x: 4, y: 4, z: 8, core: 2. Of those that a mesh axis runs over, the one named last changes fastest.
Arguments:
- trial_block: bfloat16 [128, 512, 4, 1024], P('vert', 'ma'), may hold values from -6 to 6
- legendre: bfloat16 [512, 2, 256, 1024], P('ma'), may hold values from -0.1875 to 0.1875
- order_slot: int32 [512], replicated, may hold values from 0 to 511, each once
- cycle_start: int32 [256], replicated, may hold values from 0 to 1023
- cycle_count: int32 [256], replicated, may hold values from 0 to 1024, as said below
- cycle_weight: float32 [256], replicated, may hold values from 4 to 32
Outputs:
- new_basis: bfloat16 [128, 512, 4, 1024], P('vert', 'ma')
- ritz_matrix: float32 [128, 128], replicated
Inputs may be any that keep to these rules, and one draw needn't show every extreme that they name: `cycle_count`: exactly 64 consecutive cycles have a nonzero count, and one of them has 1024.
All inputs are finite; a program needn't handle non-finite values.
Results may differ from a plain program's by a relative error of at most 0.0073.
The roundings to bfloat16 on the way count: a program that leaves them out, or rounds other values in their place, can miss the bound.
Values may be sent and summed in bfloat16 or wider, within the bound.
No kernel may reach another device: no remote copies, remote signals or barrier semaphores. Data moves between devices by JAX's collectives and lax.ppermute only.
A program may use at most 192 MiB of HBM per device.

v0:
```python
import math

import jax
import jax.numpy as jnp
from jax import lax
from jax.experimental import pallas as pl
from jax.experimental.pallas import tpu as pltpu
from jax.sharding import Mesh
from jax.sharding import PartitionSpec as P

MA = ("ma_0", "ma_1", "ma_2")
F32 = jnp.float32
BF16 = jnp.bfloat16
WINDOW = 80
PANEL = 8
COEFFICIENTS = 512 * 4 * 1024
NT = (((1,), (1,)), ((), ()))
NN = (((1,), (0,)), ((), ()))


def ring(size, shift):
    return [(i, (i + shift) % size) for i in range(size)]


def dot(a, b, dims=NN):
    return lax.dot_general(a, b, dims, preferred_element_type=F32)


def in_hbm(value):
    return pltpu.with_memory_space_constraint(value, pltpu.HBM)


def dot_high(a, b, dims=NN):
    return lax.dot_general(
        a, b, dims, precision=lax.Precision.HIGHEST, preferred_element_type=F32
    )


def window_copy(legendre, leg_v, sem, s, slot, start):
    return pltpu.make_async_copy(
        legendre.at[s, :, pl.ds(start, WINDOW), :], leg_v.at[slot], sem.at[slot]
    )


def by_part(vectors):
    shape = (4 * vectors, 4 * vectors)
    i = lax.broadcasted_iota(jnp.int32, shape, 0)
    j = lax.broadcasted_iota(jnp.int32, shape, 1)
    return (j == (i % vectors) * 4 + i // vectors).astype(BF16)


def synthesize_kernel(
    counts, trial, legendre, fields, sent1, sent2, sent3, where,
    tr_v, leg_v, one, two, prod, sem_t, sem_l, sem_o,
):
    vectors, orders = trial.shape[:2]
    me = lax.axis_index("vert")
    pair = orders // 4

    def send_copies():
        for d, out in enumerate((sent1, sent2, sent3)):
            yield pltpu.make_async_copy(
                tr_v.at[pl.ds((me + d + 1) % 4 * pair, pair)], out, sem_o.at[d]
            )

    for s in range(orders):
        pltpu.make_async_copy(trial.at[:, s], tr_v.at[s], sem_t.at[s]).start()
    live = counts[...] > 0
    cycle = lax.broadcasted_iota(jnp.int32, live.shape, 0) * live.shape[1]
    cycle = cycle + lax.broadcasted_iota(jnp.int32, live.shape, 1)
    last = legendre.shape[2] - fields.shape[0]
    first = jnp.min(jnp.where(live, cycle, last).astype(F32)).astype(jnp.int32)
    start = jnp.minimum((first // 16) * 16, legendre.shape[2] - WINDOW)
    start = pl.multiple_of(start, 16)
    shift = first - start
    where[0] = start
    where[1] = shift
    for s in range(orders):
        window_copy(legendre, leg_v, sem_l, s, s, start).start()
    for s in range(orders):
        pltpu.make_async_copy(trial.at[:, s], tr_v.at[s], sem_t.at[s]).wait()
        x = tr_v[s].reshape(4 * vectors, tr_v.shape[3])
        window_copy(legendre, leg_v, sem_l, s, s, start).wait()
        slot = s % 2
        one[slot, :, :WINDOW] = dot(x, leg_v[s, 0], NT)
        two[slot, :, :WINDOW] = dot(x, leg_v[s, 1], NT)
        w, x = (
            [ref[slot, pl.ds(c, vectors, stride=4), :] for c in range(4)]
            for ref in (one, two)
        )
        f = jnp.concatenate([w[0] + x[3], w[1] - x[2], -x[0] - w[3], x[1] - w[2]], axis=0)
        prod[s * WINDOW : (s + 1) * WINDOW] = f.T[:WINDOW]
        if s == orders - 1:
            for copy in send_copies():
                copy.start()
    for r in range(fields.shape[0]):
        fields[r] = prod[pl.ds(shift + r, orders, stride=WINDOW), :].astype(BF16)
    for copy in send_copies():
        copy.wait()


def synthesize(counts, trial, legendre, cycles):
    vectors, orders, _, degrees = trial.shape
    columns = 4 * vectors
    hbm = pl.BlockSpec(memory_space=pltpu.HBM)
    vmem = pl.BlockSpec(memory_space=pltpu.VMEM)
    sent = pltpu.HBM((orders // 4, vectors, 4, degrees), BF16)
    return pl.pallas_call(
        synthesize_kernel,
        out_shape=(
            jax.ShapeDtypeStruct((cycles, orders, columns), BF16),
            sent,
            sent,
            sent,
            jax.ShapeDtypeStruct((2,), jnp.int32),
        ),
        in_specs=[vmem, hbm, hbm],
        out_specs=(vmem, hbm, hbm, hbm, pl.BlockSpec(memory_space=pltpu.SMEM)),
        scratch_shapes=[
            pltpu.VMEM((orders, vectors, 4, degrees), BF16),
            pltpu.VMEM((orders, 2, WINDOW, degrees), BF16),
            pltpu.VMEM((2, columns, 128), F32),
            pltpu.VMEM((2, columns, 128), F32),
            pltpu.VMEM((orders * WINDOW, columns), F32),
            pltpu.SemaphoreType.DMA((orders,)),
            pltpu.SemaphoreType.DMA((orders,)),
            pltpu.SemaphoreType.DMA((3,)),
        ],
        compiler_params=pltpu.CompilerParams(vmem_limit_bytes=40 << 20),
        cost_estimate=pl.CostEstimate(
            flops=600_000_000, bytes_accessed=5 << 20, transcendentals=0
        ),
        name="synthesize",
    )(counts, in_hbm(trial), in_hbm(legendre))


def arrange_kernel(trial, tt, tr_v, tt_v, sem_t, sem_o):
    vectors, orders = trial.shape[:2]
    for s in range(orders):
        pltpu.make_async_copy(trial.at[:, s], tr_v.at[s], sem_t.at[s]).start()
    order = by_part(vectors)
    for s in range(orders):
        pltpu.make_async_copy(trial.at[:, s], tr_v.at[s], sem_t.at[s]).wait()
        t = dot(order, tr_v[s].reshape(4 * vectors, tr_v.shape[3])).astype(BF16)
        for c in range(4):
            tt_v[s, c] = t[c * vectors : (c + 1) * vectors]
        pltpu.make_async_copy(tt_v.at[s], tt.at[s], sem_o.at[s]).start()
    for s in range(orders):
        pltpu.make_async_copy(tt_v.at[s], tt.at[s], sem_o.at[s]).wait()


def arrange(trial):
    vectors, orders, _, degrees = trial.shape
    hbm = pl.BlockSpec(memory_space=pltpu.HBM)
    return pl.pallas_call(
        arrange_kernel,
        out_shape=pltpu.HBM((orders, 4, vectors, degrees), BF16),
        in_specs=[hbm],
        out_specs=hbm,
        scratch_shapes=[
            pltpu.VMEM((orders, vectors, 4, degrees), BF16),
            pltpu.VMEM((orders, 4, vectors, degrees), BF16),
            pltpu.SemaphoreType.DMA((orders,)),
            pltpu.SemaphoreType.DMA((orders,)),
        ],
        compiler_params=pltpu.CompilerParams(vmem_limit_bytes=40 << 20),
        cost_estimate=pl.CostEstimate(
            flops=300_000_000, bytes_accessed=4 << 20, transcendentals=0
        ),
        name="arrange",
    )(in_hbm(trial))


def quarter_sine(x):
    y = x * x
    sine = 1.0 + y * (-1 / 6 + y * (1 / 120 + y * (-1 / 5040 + y * (1 / 362880 + y * (-1 / 39916800)))))
    cosine = 1.0 + y * (
        -1 / 2 + y * (1 / 24 + y * (-1 / 720 + y * (1 / 40320 + y * (-1 / 3628800 + y * (1 / 479001600)))))
    )
    return sine * x, cosine


def turn(phase, longitudes):
    quarter = longitudes // 4
    s, c = quarter_sine((phase & (quarter - 1)).astype(F32) * (2.0 * math.pi / longitudes))
    quadrant = phase // quarter
    swapped = (quadrant & 1) == 1
    sine = jnp.where(swapped, c, s)
    cosine = jnp.where(swapped, s, c)
    sine = jnp.where(quadrant >= 2, -sine, sine)
    cosine = jnp.where((quadrant == 1) | (quadrant == 2), -cosine, cosine)
    return sine, cosine


def transform_kernel(
    where, begins, counts, weights, slots, received, returned, cosine, sines
):
    orders, longitudes = cosine.shape
    lanes = slots.shape[1]
    columns = received.shape[1]
    part = columns // 4
    scale = 1.0 / math.sqrt(orders)
    near = lax.broadcasted_iota(jnp.int32, (lanes, lanes), 1)
    for g in range(slots.shape[0]):
        m = jnp.broadcast_to(slots[g : g + 1, :].astype(F32), (lanes, lanes)).T
        m = m.astype(jnp.int32)
        span = slice(g * lanes, (g + 1) * lanes)
        step_s, step_c = turn((m * lanes) & (longitudes - 1), longitudes)
        s, c = turn((m * near) & (longitudes - 1), longitudes)
        s, c = s * scale, c * scale
        for b in range(longitudes // lanes):
            cosine[span, b * lanes : (b + 1) * lanes] = c.astype(BF16)
            sines[span, b * lanes : (b + 1) * lanes] = s.astype(BF16)
            s, c = s * step_c + c * step_s, c * step_c - s * step_s

    home = (lax.axis_index("ma_0") * 8 + lax.axis_index("ma_1")) * 2 + lax.axis_index("ma_2")
    r = where[0] + where[1] + home
    j = lax.broadcasted_iota(jnp.int32, (1, longitudes), 1)
    inside = ((j - begins[r]) & (longitudes - 1)) < counts[r]
    factor = jnp.where(inside, weights[r], 0.0)

    ft = received[...].astype(F32).T.astype(BF16)
    with_cos = jnp.concatenate([ft[:part], ft[3 * part :]], axis=0)
    with_sin = ft[part : 3 * part]
    grid = dot(with_cos, cosine[...]) + dot(with_sin, sines[...])
    weighted = (grid * factor).astype(BF16)
    colat, azimuth = weighted[:part], weighted[part:]
    none = jnp.zeros_like(colat)
    back = dot(
        cosine[...], jnp.concatenate([colat, none, none, azimuth], axis=0), NT
    ) + dot(sines[...], jnp.concatenate([none, colat, azimuth, none], axis=0), NT)
    returned[...] = back.astype(BF16)


def cycle_transform(where, begins, counts, weights, slots, received):
    vmem = pl.BlockSpec(memory_space=pltpu.VMEM)
    smem = pl.BlockSpec(memory_space=pltpu.SMEM)
    orders = slots.size
    return pl.pallas_call(
        transform_kernel,
        out_shape=jax.ShapeDtypeStruct(received.shape, BF16),
        in_specs=[smem] * 4 + [vmem] * 2,
        out_specs=vmem,
        scratch_shapes=[pltpu.VMEM((orders, 2 * orders), BF16)] * 2,
        compiler_params=pltpu.CompilerParams(vmem_limit_bytes=40 << 20),
        cost_estimate=pl.CostEstimate(
            flops=600_000_000, bytes_accessed=3 << 20, transcendentals=0
        ),
        name="transform",
    )(where, begins, counts, weights, slots, received)


def trial_gram_kernel(
    trial, block1, block2, block3, own, home1, home2, home3, mine, sem
):
    n, _, _, degrees = trial.shape
    me = lax.axis_index("vert")
    copies = [
        pltpu.make_async_copy(trial.at[:, 2 * me + i], mine.at[i], sem.at[i]) for i in range(2)
    ]
    for copy in copies:
        copy.start()
    order = by_part(n)
    total = 0.0
    for i in range(2):
        copies[i].wait()
        parts = [
            dot(order, b.reshape(4 * n, degrees)).astype(BF16)
            for b in (mine[i], block1[i], block2[i], block3[i])
        ]
        for c in range(4):
            x = jnp.concatenate([p[c * n : (c + 1) * n] for p in parts], axis=0)
            total = total + dot(x, x, NT)
    for d, out in enumerate((own, home1, home2, home3)):
        rows = total[d * n : (d + 1) * n]
        out[...] = jnp.concatenate(
            [rows[:, (d - e) % 4 * n : ((d - e) % 4 + 1) * n] for e in range(4)], axis=1
        )


def trial_gram(trial, received):
    vectors, _, parts, degrees = trial.shape
    vmem = pl.BlockSpec(memory_space=pltpu.VMEM)
    return pl.pallas_call(
        trial_gram_kernel,
        out_shape=[jax.ShapeDtypeStruct((vectors, 4 * vectors), F32)] * 4,
        in_specs=[pl.BlockSpec(memory_space=pltpu.HBM)] + [vmem] * 3,
        scratch_shapes=[
            pltpu.VMEM((2, vectors, parts, degrees), BF16),
            pltpu.SemaphoreType.DMA((2,)),
        ],
        compiler_params=pltpu.CompilerParams(vmem_limit_bytes=32 << 20),
        cost_estimate=pl.CostEstimate(
            flops=600_000_000, bytes_accessed=2 << 20, transcendentals=0
        ),
        name="trial_gram",
    )(in_hbm(trial), *received)


def analyse_kernel(
    where, got0, got1, got2, got3, rows0, rows1, rows2, rows3, legendre,
    tt, applied, gram,
    got_v, rows_v, wide, adj, leg_v, tt_v, sem_g, sem_r, sem_l, sem_t,
):
    orders, _, vectors, _ = tt.shape
    columns = 4 * vectors
    start = pl.multiple_of(where[0], 16)
    shift = where[1]

    def trial_copy(n):
        return pltpu.make_async_copy(tt.at[n], tt_v.at[n], sem_t.at[n])

    got_copies = [
        pltpu.make_async_copy(got, got_v.at[e], sem_g.at[e])
        for e, got in enumerate((got0, got1, got2, got3))
    ]
    row_copies = [
        pltpu.make_async_copy(rows, rows_v.at[e], sem_r.at[e])
        for e, rows in enumerate((rows0, rows1, rows2, rows3))
    ]
    for copy in got_copies:
        copy.start()
    for n in range(orders):
        window_copy(legendre, leg_v, sem_l, n, n, start).start()
        trial_copy(n).start()
    for copy in row_copies:
        copy.start()
    for e, copy in enumerate(got_copies):
        copy.wait()
        wide[e] = got_v[e].astype(F32)
    adj[...] = jnp.zeros_like(adj)
    lane = lax.broadcasted_iota(jnp.int32, (1, columns), 1) // vectors
    one = jnp.ones((1, columns), F32)
    sign0 = jnp.where(lane < 2, one, -one)
    sign1 = jnp.where((lane == 0) | (lane == 3), -one, one)
    cycles = got0.shape[0] // orders
    block = {0: 0, 1: 1, 3: 2, 2: 3}
    total = 0.0
    for n in range(orders):
        for e in range(4):
            x = wide[e, pl.ds(n, cycles, stride=orders), :]
            base = e * 2 * WINDOW + shift
            adj[pl.ds(base, cycles), :] = x * sign0
            adj[pl.ds(base + WINDOW, cycles), :] = pltpu.roll(x, columns // 2, 1) * sign1
        a = jnp.concatenate(
            [adj[e * 2 * WINDOW : (e + 1) * 2 * WINDOW].T for e in range(4)], axis=0
        ).astype(BF16)
        window_copy(legendre, leg_v, sem_l, n, n, start).wait()
        rows = dot(a, leg_v[n].reshape(2 * WINDOW, leg_v.shape[3])).astype(BF16)
        trial_copy(n).wait()
        for c in range(4):
            b = block[c] * vectors
            own = [rows[e * columns + b : e * columns + b + vectors] for e in range(4)]
            every = jnp.concatenate(own, axis=0)
            applied[n, c] = every
            total = total + dot(every, jnp.concatenate([tt_v[n, c], own[0]], axis=0), NT)
    for copy in row_copies:
        copy.wait()
    gram[:vectors] = (rows_v[0] + rows_v[1]) + (rows_v[2] + rows_v[3])
    gram[vectors:] = total.T


def analyse(where, gots, trial_rows, legendre, tt):
    orders, _, vectors, degrees = tt.shape
    cycles_rows, columns = gots[0].shape
    vmem = pl.BlockSpec(memory_space=pltpu.VMEM)
    hbm = pl.BlockSpec(memory_space=pltpu.HBM)
    return pl.pallas_call(
        analyse_kernel,
        out_shape=(
            jax.ShapeDtypeStruct((orders, 4, 4 * vectors, degrees), BF16),
            jax.ShapeDtypeStruct((3 * vectors, 4 * vectors), F32),
        ),
        in_specs=[pl.BlockSpec(memory_space=pltpu.SMEM)] + [hbm] * 10,
        out_specs=(vmem, vmem),
        scratch_shapes=[
            pltpu.VMEM((4, cycles_rows, columns), BF16),
            pltpu.VMEM((4, vectors, columns), F32),
            pltpu.VMEM((4, cycles_rows, columns), F32),
            pltpu.VMEM((4 * 2 * WINDOW, columns), F32),
            pltpu.VMEM((orders, 2, WINDOW, degrees), BF16),
            pltpu.VMEM((orders, 4, vectors, degrees), BF16),
            pltpu.SemaphoreType.DMA((4,)),
            pltpu.SemaphoreType.DMA((4,)),
            pltpu.SemaphoreType.DMA((orders,)),
            pltpu.SemaphoreType.DMA((orders,)),
        ],
        compiler_params=pltpu.CompilerParams(vmem_limit_bytes=40 << 20),
        cost_estimate=pl.CostEstimate(
            flops=2_000_000_000, bytes_accessed=14 << 20, transcendentals=0
        ),
        name="analyse",
    )(where, *gots, *trial_rows, in_hbm(legendre), in_hbm(tt))


def eliminate(work, n):
    shape = (PANEL, n)
    sub = lax.broadcasted_iota(jnp.int32, shape, 0)
    for j in range(0, n, PANEL):
        for which in range(work.shape[0]):
            top = work[which, j : j + PANEL, :n]
            value, low, inverse = {}, {}, []
            for m in range(PANEL):
                column = jnp.broadcast_to(top[:, j + m : j + m + 1], shape)
                for i in range(m, PANEL):
                    value[i, m] = jnp.broadcast_to(column[i : i + 1], shape)
            for m in range(PANEL):
                inverse.append(lax.rsqrt(value[m, m]))
                for i in range(m + 1, PANEL):
                    low[i, m] = value[i, m] * inverse[m]
                for i in range(m + 1, PANEL):
                    for k in range(m + 1, i + 1):
                        value[i, k] = value[i, k] - low[i, m] * low[k, m]

            def solved(base):
                rows = []
                for m in range(PANEL):
                    line = jnp.broadcast_to(
                        work[which, j + m : j + m + 1, base : base + n], shape
                    )
                    for k in range(m):
                        line = line - low[m, k] * rows[k]
                    rows.append(line * inverse[m])
                return rows

            left = solved(0) if j + PANEL < n else None
            right = solved(n)
            panel = right[0]
            for m in range(1, PANEL):
                panel = jnp.where(sub == m, right[m], panel)
            work[which, j : j + PANEL, n:] = panel
            for i in range(j + PANEL, n, PANEL):
                block = work[which, i : i + PANEL, :n]
                tail = work[which, i : i + PANEL, n:]
                factor = []
                for m in range(PANEL):
                    column = jnp.broadcast_to(block[:, j + m : j + m + 1], shape)
                    for k in range(m):
                        column = column - low[m, k] * factor[k]
                    factor.append(column * inverse[m])
                for m in range(PANEL):
                    block = block - factor[m] * left[m]
                    tail = tail - factor[m] * right[m]
                work[which, i : i + PANEL, :n] = block
                work[which, i : i + PANEL, n:] = tail


def factors_kernel(
    grams, weights, ritz, gram_v, work, cross, sem
):
    n = cross.shape[0]
    vectors = n // 4
    copies = [
        pltpu.make_async_copy(grams.at[group], gram_v.at[group], sem.at[group])
        for group in range(grams.shape[0])
    ]
    for copy in copies:
        copy.start()
    me = lax.axis_index("vert")
    unit = (
        lax.broadcasted_iota(jnp.int32, (n, n), 0)
        == lax.broadcasted_iota(jnp.int32, (n, n), 1)
    ).astype(F32)
    work[0, :, n:] = unit
    work[1, :, n:] = unit
    for group, copy in enumerate(copies):
        copy.wait()
        rows = gram_v[group] * (1.0 / COEFFICIENTS)
        if group:
            rows = pltpu.roll(rows, group * vectors, 1)
        span = pl.ds(group * vectors, vectors)
        work[0, span, :n] = rows[:vectors]
        cross[span, :] = rows[vectors : 2 * vectors]
        work[1, span, :n] = rows[2 * vectors :]
    eliminate(work, n)
    inverse_trial = work[0, :, n:]
    ritz[...] = dot_high(dot_high(inverse_trial, cross[...]), inverse_trial, NT)
    mine = work[1, pl.ds(pl.multiple_of(me * vectors, vectors), vectors), n:]
    mine = pltpu.roll(mine, ((4 - me) & 3) * vectors, 1).astype(BF16)
    i = lax.broadcasted_iota(jnp.int32, (n, vectors), 0)
    repeat = (i // 4 == lax.broadcasted_iota(jnp.int32, (n, vectors), 1)).astype(BF16)
    mine = dot(repeat, mine)
    part = lax.broadcasted_iota(jnp.int32, (n, n), 0) & 3
    weights[...] = jnp.concatenate(
        [jnp.where(part == c, mine, 0.0) for c in range(4)], axis=1
    ).astype(BF16)


def factors(grams):
    _, rows, n = grams.shape
    vmem = pl.BlockSpec(memory_space=pltpu.VMEM)
    return pl.pallas_call(
        factors_kernel,
        out_shape=(
            jax.ShapeDtypeStruct((n, 4 * n), BF16),
            jax.ShapeDtypeStruct((n, n), F32),
        ),
        in_specs=[pl.BlockSpec(memory_space=pltpu.HBM)],
        out_specs=(vmem, vmem),
        scratch_shapes=[
            pltpu.VMEM((4, rows, n), F32),
            pltpu.VMEM((2, n, 2 * n), F32),
            pltpu.VMEM((n, n), F32),
            pltpu.SemaphoreType.DMA((4,)),
        ],
        compiler_params=pltpu.CompilerParams(vmem_limit_bytes=16 << 20),
        cost_estimate=pl.CostEstimate(
            flops=100_000_000, bytes_accessed=1 << 20, transcendentals=0
        ),
        name="factors",
    )(grams)


def mix_kernel(weights, applied, new_basis, out_v, sem):
    orders, parts, n, degrees = applied.shape
    for s in range(orders):
        y = dot(weights[...], applied[s].reshape(parts * n, degrees)).astype(BF16)
        out_v[s] = y.reshape(n // 4, 4, degrees)
        pltpu.make_async_copy(out_v.at[s], new_basis.at[:, s], sem.at[s]).start()
    for s in range(orders):
        pltpu.make_async_copy(out_v.at[s], new_basis.at[:, s], sem.at[s]).wait()


def mix(weights, applied):
    orders, _, n, degrees = applied.shape
    vmem = pl.BlockSpec(memory_space=pltpu.VMEM)
    return pl.pallas_call(
        mix_kernel,
        out_shape=pltpu.HBM((n // 4, orders, 4, degrees), BF16),
        in_specs=[vmem, vmem],
        out_specs=pl.BlockSpec(memory_space=pltpu.HBM),
        scratch_shapes=[
            pltpu.VMEM((orders, n // 4, 4, degrees), BF16),
            pltpu.SemaphoreType.DMA((orders,)),
        ],
        compiler_params=pltpu.CompilerParams(vmem_limit_bytes=32 << 20),
        cost_estimate=pl.CostEstimate(
            flops=1_100_000_000, bytes_accessed=10 << 20, transcendentals=0
        ),
        name="mix",
    )(weights, applied)


def swap(value, axis, size, bit):
    return lax.ppermute(value, axis, [(i, i ^ bit) for i in range(size)])


def sum_of_four(value, axis, size):
    one, two, three = (swap(value, axis, size, bit) for bit in (1, 2, 3))
    return (value + one) + (two + three)


def sum_over_ma(value):
    value = value + swap(value, "ma_2", 2, 1)
    value = sum_of_four(value, "ma_1", 8)
    value = value + swap(value, "ma_1", 8, 4)
    return sum_of_four(value, "ma_0", 4)


def from_groups(value):
    return [value] + [lax.ppermute(value, "vert", ring(4, -d)) for d in (1, 2, 3)]


def shards(trial_block, legendre, order_slot, cycle_start, cycle_count, cycle_weight):
    vectors, orders, _, _ = trial_block.shape
    live = legendre.shape[2] // 4
    columns = 4 * vectors

    fields, *sent, where = synthesize(
        cycle_count.reshape(-1, 128), trial_block, legendre, live
    )
    blocks = [lax.ppermute(x, "vert", ring(4, d)) for d, x in enumerate(sent, 1)]
    received = lax.all_to_all(fields, MA, split_axis=0, concat_axis=0, tiled=True)
    tt = arrange(trial_block)
    received, tt = lax.optimization_barrier((received, tt))
    returned = cycle_transform(
        where, cycle_start, cycle_count, cycle_weight, order_slot.reshape(-1, 128),
        received.reshape(live * orders, columns),
    )
    order_fields = lax.all_to_all(
        returned.reshape(live, orders, columns), MA, split_axis=0, concat_axis=0, tiled=True
    )
    shares = trial_gram(trial_block, blocks)
    trial_rows = [shares[0]] + [
        lax.ppermute(shares[d], "vert", ring(4, -d)) for d in (1, 2, 3)
    ]
    order_fields, *trial_rows = lax.optimization_barrier((order_fields, *trial_rows))
    gots = from_groups(order_fields.reshape(live * orders, columns))
    applied, gram = analyse(where, gots, trial_rows, legendre, tt)
    summed = jnp.broadcast_to(sum_over_ma(gram)[None], (4, *gram.shape))
    grams = lax.all_to_all(summed, "vert", split_axis=0, concat_axis=0, tiled=True)
    weights, ritz_matrix = factors(grams)
    return (mix(weights, applied), ritz_matrix)


def solution(mesh):
    split = Mesh(
        mesh.devices.reshape(4, 8, 2, mesh.shape["vert"]), ("ma_0", "ma_1", "ma_2", "vert")
    )
    placed = (P("vert", MA, None, None), P(MA, None, None, None), P(), P(), P(), P())
    return jax.shard_map(
        shards,
        mesh=split,
        in_specs=placed,
        out_specs=(P("vert", MA, None, None), P()),
        check_vma=False,
    )
```

profile of v0, /device:TPU:64, one launch (start us, length us, event | category | flops | bytes accessed | tf_op | source)
XLA Modules:
  0.0 123.6 jit_solution(508143371041816230)
XLA Ops:
  0.6 0.7 copy-done
  1.3 6.5 %synthesize.1 = (bf16[64,8,128]{2,1,0:T(8,128)(2,1)}, bf16[2,32,4,1024]{3,2,1,0:T(4,128)(2,1)}, bf16[2,32,4,1024]{3,2,1,0:T(4,128)(2,1)}, bf16[2,32,4,1024]{3,2,1,0:T(4,128)(2,1)}, s32[2]{0:T(128)S(1)}) custom-call(s32[2,128]{1,0:T(2,128)S(1)} %bitcast.10, bf16[32,8,4,1024]{3,2,1,0:T(4,128)(2,1)} %trial.5, bf16[8,2,256,1024]{3,2,1,0:T(8,128)(2,1)} %legendre.3), custom_call_target="tpu_custom_call" | custom-call | flops 600000000 | bytes 5242880 | tf_op jit(solution)/shard_map/synthesize/pallas_call | solution.py:108
  7.8 1.6 %collective-permute-start = (bf16[2,32,4,1024]{3,2,1,0:T(4,128)(2,1)}, bf16[2,32,4,1024]{3,2,1,0:T(4,128)(2,1)S(1)}, u32[]{:S(2)}, u32[]{:S(2)}) collective-permute-start(bf16[2,32,4,1024]{3,2,1,0:T(4,128)(2,1)} %get-tuple-element.25), channel_id=1, source_target_pairs={{0,1},{1,2},{2,3},{3,0},{4,5},{5,6},{6,7},{7,4},{8,9},{9,10},{10,1... | collective-permute-start | bytes 1572872 | tf_op jit(solution)/shard_map/ppermute | solution.py:572
  9.4 2.7 %collective-permute-start.1 = (bf16[2,32,4,1024]{3,2,1,0:T(4,128)(2,1)}, bf16[2,32,4,1024]{3,2,1,0:T(4,128)(2,1)S(1)}, u32[]{:S(2)}, u32[]{:S(2)}) collective-permute-start(bf16[2,32,4,1024]{3,2,1,0:T(4,128)(2,1)} %get-tuple-element.26), channel_id=1, source_target_pairs={{0,2},{1,3},{2,0},{3,1},{4,6},{5,7},{6,4},{7,5},{8,10},{9,11},{10,... | collective-permute-start | bytes 1572872 | tf_op jit(solution)/shard_map/ppermute | solution.py:572
  12.1 1.4 %collective-permute-start.2 = (bf16[2,32,4,1024]{3,2,1,0:T(4,128)(2,1)}, bf16[2,32,4,1024]{3,2,1,0:T(4,128)(2,1)S(1)}, u32[]{:S(2)}, u32[]{:S(2)}) collective-permute-start(bf16[2,32,4,1024]{3,2,1,0:T(4,128)(2,1)} %get-tuple-element.27), channel_id=1, source_target_pairs={{0,3},{1,0},{2,1},{3,2},{4,7},{5,4},{6,5},{7,6},{8,11},{9,8},{10,9... | collective-permute-start | bytes 1572872 | tf_op jit(solution)/shard_map/ppermute | solution.py:572
  13.5 11.3 %all-to-all-start = ((bf16[64,8,128]{2,1,0:T(8,128)(2,1)}), bf16[64,8,128]{2,1,0:T(8,128)(2,1)S(1)}, u32[]{:S(2)}, u32[]{:S(2)}) async-start(bf16[64,8,128]{2,1,0:T(8,128)(2,1)} %get-tuple-element.23), calls=%async_computation | async-start | bytes 262144 | tf_op jit(solution)/shard_map/all_to_all | solution.py:573
  24.9 3.6 %arrange.1.tt = bf16[8,4,32,1024]{3,2,1,0:T(8,128)(2,1)} custom-call(bf16[32,8,4,1024]{3,2,1,0:T(4,128)(2,1)} %trial.5), custom_call_target="tpu_custom_call" | custom-call | flops 300000000 | bytes 4194304 | tf_op jit(solution)/shard_map/arrange/pallas_call | solution.py:155
  28.4 5.7 %all-to-all-done = bf16[64,8,128]{2,1,0:T(8,128)(2,1)S(1)} async-done(((bf16[64,8,128]{2,1,0:T(8,128)(2,1)}), bf16[64,8,128]{2,1,0:T(8,128)(2,1)S(1)}, u32[]{:S(2)}, u32[]{:S(2)}) %all-to-all-start) | async-done | bytes 131104 | tf_op jit(solution)/shard_map/all_to_all | solution.py:573
  34.2 4.0 %transform.1 = bf16[512,128]{1,0:T(8,128)(2,1)} custom-call(s32[2]{0:T(128)S(1)} %get-tuple-element.22.where, s32[256]{0:T(256)S(1)} %copy-done.3, s32[256]{0:T(256)S(1)} %copy-done.1, f32[256]{0:T(256)S(1)} %copy-done.4, s32[4,128]{1,0:T(4,128)S(1)} %bitcast.11, bf16[512,128]{1,0:T(8,128)(2,1)S(1)} %bitcast.9), custom_call_target="tpu_custom_call" | custom-call | flops 600000000 | bytes 3145728 | tf_op jit(solution)/shard_map/transform/pallas_call | solution.py:239
  38.2 5.9 %all-to-all-start.1 = ((bf16[64,8,128]{2,1,0:T(8,128)(2,1)}), bf16[64,8,128]{2,1,0:T(8,128)(2,1)S(1)}, u32[]{:S(2)}, u32[]{:S(2)}) async-start(bf16[64,8,128]{2,1,0:T(8,128)(2,1)} %bitcast.3), calls=%async_computation.1 | async-start | bytes 262144 | tf_op jit(solution)/shard_map/all_to_all | solution.py:580
  44.1 3.4 %trial_gram.1 = (f32[32,128]{1,0:T(8,128)S(1)}, f32[32,128]{1,0:T(8,128)S(1)}, f32[32,128]{1,0:T(8,128)S(1)}, f32[32,128]{1,0:T(8,128)S(1)}) custom-call(bf16[32,8,4,1024]{3,2,1,0:T(4,128)(2,1)} %trial.5, bf16[2,32,4,1024]{3,2,1,0:T(4,128)(2,1)S(1)} %collective-permute-done.block1, bf16[2,32,4,1024]{3,2,1,0:T(4,128)(2,1)S(1)} %collective-permute-done.1.block2, ...), custom_call_target="tpu_custom_call" | custom-call | flops 600000000 | bytes 2097152 | tf_op jit(solution)/shard_map/trial_gram/pallas_call | solution.py:284
  47.6 2.7 %collective-permute-start.4 = (f32[32,128]{1,0:T(8,128)S(1)}, f32[32,128]{1,0:T(8,128)S(1)}, u32[]{:S(2)}, u32[]{:S(2)}) collective-permute-start(f32[32,128]{1,0:T(8,128)S(1)} %get-tuple-element.30), channel_id=1, source_target_pairs={{0,2},{1,3},{2,0},{3,1},{4,6},{5,7},{6,4},{7,5},{8,10},{9,11},{10,... | collective-permute-start | bytes 49160 | tf_op jit(solution)/shard_map/ppermute | solution.py:585
  50.3 3.2 %all-to-all-done.1 = bf16[64,8,128]{2,1,0:T(8,128)(2,1)S(1)} async-done(((bf16[64,8,128]{2,1,0:T(8,128)(2,1)}), bf16[64,8,128]{2,1,0:T(8,128)(2,1)S(1)}, u32[]{:S(2)}, u32[]{:S(2)}) %all-to-all-start.1) | async-done | bytes 131104 | tf_op jit(solution)/shard_map/all_to_all | solution.py:580
  53.5 1.7 %collective-permute-done.5.rows3 = f32[32,128]{1,0:T(8,128)S(1)} collective-permute-done((f32[32,128]{1,0:T(8,128)S(1)}, f32[32,128]{1,0:T(8,128)S(1)}, u32[]{:S(2)}, u32[]{:S(2)}) %collective-permute-start.5) | collective-permute-done | bytes 16416 | tf_op jit(solution)/shard_map/ppermute | solution.py:585
  55.2 2.3 %collective-permute-start.7 = (bf16[512,128]{1,0:T(8,128)(2,1)S(1)}, bf16[512,128]{1,0:T(8,128)(2,1)S(1)}, u32[]{:S(2)}, u32[]{:S(2)}) collective-permute-start(bf16[512,128]{1,0:T(8,128)(2,1)S(1)} %bitcast.6), channel_id=1, source_target_pairs={{0,2},{1,3},{2,0},{3,1},{4,6},{5,7},{6,4},{7,5},{8,10},{9,11},{10,... | collective-permute-start | bytes 393224 | tf_op jit(solution)/shard_map/ppermute | solution.py:561
  57.5 1.0 collective-permute-start.6
  58.5 4.6 %collective-permute-done.8.got3 = bf16[512,128]{1,0:T(8,128)(2,1)S(1)} collective-permute-done((bf16[512,128]{1,0:T(8,128)(2,1)S(1)}, bf16[512,128]{1,0:T(8,128)(2,1)S(1)}, u32[]{:S(2)}, u32[]{:S(2)}) %collective-permute-start.8) | collective-permute-done | bytes 131104 | tf_op jit(solution)/shard_map/ppermute | solution.py:561
  63.8 13.3 %analyse.1 = (bf16[8,4,128,1024]{3,2,1,0:T(8,128)(2,1)S(1)}, f32[96,128]{1,0:T(8,128)S(1)}) custom-call(s32[2]{0:T(128)S(1)} %get-tuple-element.22.where, bf16[512,128]{1,0:T(8,128)(2,1)S(1)} %bitcast.8, bf16[512,128]{1,0:T(8,128)(2,1)S(1)} %collective-permute-done.6.got1, bf16[512,128]{1,0:T(8,128)(2,1)S(1)} %collective-permute-done.7.got2, ...), custom_call_target="tpu_custom_call" | custom-call | flops 2000000000 | bytes 14680064 | tf_op jit(solution)/shard_map/analyse/pallas_call | solution.py:368
  77.2 1.2 collective-permute-done.9
  78.4 1.3 %collective-permute-start.12 = (f32[96,128]{1,0:T(8,128)S(1)}, f32[96,128]{1,0:T(8,128)S(1)}, u32[]{:S(2)}, u32[]{:S(2)}) collective-permute-start(f32[96,128]{1,0:T(8,128)S(1)} %add.24), channel_id=1, source_target_pairs={{0,24},{8,16},{16,8},{24,0},{32,56},{40,48},{48,40},{56,32},{1,25}... | collective-permute-start | bytes 147464 | tf_op jit(solution)/shard_map/ppermute | solution.py:545
  79.7 2.6 %collective-permute-start.11 = (f32[96,128]{1,0:T(8,128)S(1)}, f32[96,128]{1,0:T(8,128)S(1)}, u32[]{:S(2)}, u32[]{:S(2)}) collective-permute-start(f32[96,128]{1,0:T(8,128)S(1)} %add.24), channel_id=1, source_target_pairs={{0,16},{8,24},{16,0},{24,8},{32,48},{40,56},{48,32},{56,40},{1,17}... | collective-permute-start | bytes 147464 | tf_op jit(solution)/shard_map/ppermute | solution.py:545
  82.3 1.2 collective-permute-done.12
  83.5 2.0 %collective-permute-done.11 = f32[96,128]{1,0:T(8,128)S(1)} collective-permute-done((f32[96,128]{1,0:T(8,128)S(1)}, f32[96,128]{1,0:T(8,128)S(1)}, u32[]{:S(2)}, u32[]{:S(2)}) %collective-permute-start.11) | collective-permute-done | bytes 49184 | tf_op jit(solution)/shard_map/ppermute | solution.py:545
  85.5 0.8 collective-permute-done.10
  86.4 3.4 %collective-permute-start.13 = (f32[96,128]{1,0:T(8,128)S(1)}, f32[96,128]{1,0:T(8,128)S(1)}, u32[]{:S(2)}, u32[]{:S(2)}) collective-permute-start(f32[96,128]{1,0:T(8,128)S(1)} %add_add_fusion.1), channel_id=1, source_target_pairs={{0,32},{8,40},{16,48},{24,56},{32,0},{40,8},{48,16},{56,24},{1,33}... | collective-permute-start | bytes 147464 | tf_op jit(solution)/shard_map/ppermute | solution.py:545
  89.8 5.0 %collective-permute-done.13 = f32[96,128]{1,0:T(8,128)S(1)} collective-permute-done((f32[96,128]{1,0:T(8,128)S(1)}, f32[96,128]{1,0:T(8,128)S(1)}, u32[]{:S(2)}, u32[]{:S(2)}) %collective-permute-start.13) | collective-permute-done | bytes 49184 | tf_op jit(solution)/shard_map/ppermute | solution.py:545
  94.8 3.2 %collective-permute-start.16 = (f32[96,128]{1,0:T(8,128)S(1)}, f32[96,128]{1,0:T(8,128)S(1)}, u32[]{:S(2)}, u32[]{:S(2)}) collective-permute-start(f32[96,128]{1,0:T(8,128)S(1)} %add.28), channel_id=1, source_target_pairs={{0,192},{64,128},{128,64},{192,0},{1,193},{65,129},{129,65},{193,1... | collective-permute-start | bytes 147464 | tf_op jit(solution)/shard_map/ppermute | solution.py:545
  98.9 1.2 collective-permute-done.16
  100.1 3.4 %collective-permute-done.15 = f32[96,128]{1,0:T(8,128)S(1)} collective-permute-done((f32[96,128]{1,0:T(8,128)S(1)}, f32[96,128]{1,0:T(8,128)S(1)}, u32[]{:S(2)}, u32[]{:S(2)}) %collective-permute-start.15) | collective-permute-done | bytes 49184 | tf_op jit(solution)/shard_map/ppermute | solution.py:545
  103.6 9.7 %all_to_all.15.grams = f32[4,96,128]{2,1,0:T(8,128)S(1)} all-to-all(f32[4,96,128]{2,1,0:T(8,128)S(1)} %broadcast_in_dim.2), channel_id=1, replica_groups=mesh['ma_0'=4,'ma_1'=8,'ma_2'=2,'vert'=4] {'vert'}, dimensions={0} | all-to-all | bytes 393216 | tf_op jit(solution)/shard_map/all_to_all | solution.py:591
  113.3 7.9 %factors.1 = (bf16[128,512]{1,0:T(8,128)(2,1)S(1)}, f32[128,128]{1,0:T(8,128)}) custom-call(f32[4,96,128]{2,1,0:T(8,128)S(1)} %all_to_all.15.grams), custom_call_target="tpu_custom_call" | custom-call | flops 100000000 | bytes 1048576 | tf_op jit(solution)/shard_map/factors/pallas_call | solution.py:492
  121.2 2.2 %mix.1 = bf16[32,8,4,1024]{3,2,1,0:T(4,128)(2,1)} custom-call(bf16[128,512]{1,0:T(8,128)(2,1)S(1)} %get-tuple-element.39.weights, bf16[8,4,128,1024]{3,2,1,0:T(8,128)(2,1)S(1)} %get-tuple-element.40.applied), custom_call_target="tpu_custom_call" | custom-call | flops 1100000000 | bytes 10485760 | tf_op jit(solution)/shard_map/mix/pallas_call | solution.py:527
  (29 shorter events, 1.9 us)
Async XLA Ops:
  0.6 0.7 copy-start
  7.8 36.3 %collective-permute-start = (bf16[2,32,4,1024]{3,2,1,0:T(4,128)(2,1)}, bf16[2,32,4,1024]{3,2,1,0:T(4,128)(2,1)S(1)}, u32[]{:S(2)}, u32[]{:S(2)}) collective-permute-start(bf16[2,32,4,1024]{3,2,1,0:T(4,128)(2,1)} %get-tuple-element.25), channel_id=1, source_target_pairs={{0,1},{1,2},{2,3},{3,0},{4,5},{5,6},{6,7},{7,4},{8,9},{9,10},{10,1... | collective-permute-start | bytes 1572872 | tf_op jit(solution)/shard_map/ppermute | solution.py:572
  9.4 34.8 %collective-permute-start.1 = (bf16[2,32,4,1024]{3,2,1,0:T(4,128)(2,1)}, bf16[2,32,4,1024]{3,2,1,0:T(4,128)(2,1)S(1)}, u32[]{:S(2)}, u32[]{:S(2)}) collective-permute-start(bf16[2,32,4,1024]{3,2,1,0:T(4,128)(2,1)} %get-tuple-element.26), channel_id=1, source_target_pairs={{0,2},{1,3},{2,0},{3,1},{4,6},{5,7},{6,4},{7,5},{8,10},{9,11},{10,... | collective-permute-start | bytes 1572872 | tf_op jit(solution)/shard_map/ppermute | solution.py:572
  12.1 32.1 %collective-permute-start.2 = (bf16[2,32,4,1024]{3,2,1,0:T(4,128)(2,1)}, bf16[2,32,4,1024]{3,2,1,0:T(4,128)(2,1)S(1)}, u32[]{:S(2)}, u32[]{:S(2)}) collective-permute-start(bf16[2,32,4,1024]{3,2,1,0:T(4,128)(2,1)} %get-tuple-element.27), channel_id=1, source_target_pairs={{0,3},{1,0},{2,1},{3,2},{4,7},{5,4},{6,5},{7,6},{8,11},{9,8},{10,9... | collective-permute-start | bytes 1572872 | tf_op jit(solution)/shard_map/ppermute | solution.py:572
  13.5 20.7 %all-to-all-start = ((bf16[64,8,128]{2,1,0:T(8,128)(2,1)}), bf16[64,8,128]{2,1,0:T(8,128)(2,1)S(1)}, u32[]{:S(2)}, u32[]{:S(2)}) async-start(bf16[64,8,128]{2,1,0:T(8,128)(2,1)} %get-tuple-element.23), calls=%async_computation | async-start | bytes 262144 | tf_op jit(solution)/shard_map/all_to_all | solution.py:573
  24.8 9.4 %copy-start.1 = (s32[256]{0:T(256)S(1)}, s32[256]{0:T(256)}, u32[]{:S(2)}) copy-start(s32[256]{0:T(256)} %counts.1) | copy-start | bytes 3076
  24.8 9.4 %copy-start.2 = (s32[512]{0:T(512)S(1)}, s32[512]{0:T(512)}, u32[]{:S(2)}) copy-start(s32[512]{0:T(512)} %param.8) | copy-start | bytes 6148
  24.9 9.3 %copy-start.3 = (s32[256]{0:T(256)S(1)}, s32[256]{0:T(256)}, u32[]{:S(2)}) copy-start(s32[256]{0:T(256)} %begins.1) | copy-start | bytes 3076
  24.9 9.3 %copy-start.4 = (f32[256]{0:T(256)S(1)}, f32[256]{0:T(256)}, u32[]{:S(2)}) copy-start(f32[256]{0:T(256)} %weights.1) | copy-start | bytes 3076
  38.2 15.2 %all-to-all-start.1 = ((bf16[64,8,128]{2,1,0:T(8,128)(2,1)}), bf16[64,8,128]{2,1,0:T(8,128)(2,1)S(1)}, u32[]{:S(2)}, u32[]{:S(2)}) async-start(bf16[64,8,128]{2,1,0:T(8,128)(2,1)} %bitcast.3), calls=%async_computation.1 | async-start | bytes 262144 | tf_op jit(solution)/shard_map/all_to_all | solution.py:580
  47.5 6.0 %collective-permute-start.3 = (f32[32,128]{1,0:T(8,128)S(1)}, f32[32,128]{1,0:T(8,128)S(1)}, u32[]{:S(2)}, u32[]{:S(2)}) collective-permute-start(f32[32,128]{1,0:T(8,128)S(1)} %get-tuple-element.29), channel_id=1, source_target_pairs={{0,3},{1,0},{2,1},{3,2},{4,7},{5,4},{6,5},{7,6},{8,11},{9,8},{10,9... | collective-permute-start | bytes 49160 | tf_op jit(solution)/shard_map/ppermute | solution.py:585
  47.6 5.9 %collective-permute-start.4 = (f32[32,128]{1,0:T(8,128)S(1)}, f32[32,128]{1,0:T(8,128)S(1)}, u32[]{:S(2)}, u32[]{:S(2)}) collective-permute-start(f32[32,128]{1,0:T(8,128)S(1)} %get-tuple-element.30), channel_id=1, source_target_pairs={{0,2},{1,3},{2,0},{3,1},{4,6},{5,7},{6,4},{7,5},{8,10},{9,11},{10,... | collective-permute-start | bytes 49160 | tf_op jit(solution)/shard_map/ppermute | solution.py:585
  50.3 4.9 %collective-permute-start.5 = (f32[32,128]{1,0:T(8,128)S(1)}, f32[32,128]{1,0:T(8,128)S(1)}, u32[]{:S(2)}, u32[]{:S(2)}) collective-permute-start(f32[32,128]{1,0:T(8,128)S(1)} %get-tuple-element.31), channel_id=1, source_target_pairs={{0,1},{1,2},{2,3},{3,0},{4,5},{5,6},{6,7},{7,4},{8,9},{9,10},{10,1... | collective-permute-start | bytes 49160 | tf_op jit(solution)/shard_map/ppermute | solution.py:585
  55.2 7.9 %collective-permute-start.8 = (bf16[512,128]{1,0:T(8,128)(2,1)S(1)}, bf16[512,128]{1,0:T(8,128)(2,1)S(1)}, u32[]{:S(2)}, u32[]{:S(2)}) collective-permute-start(bf16[512,128]{1,0:T(8,128)(2,1)S(1)} %bitcast.5), channel_id=1, source_target_pairs={{0,1},{1,2},{2,3},{3,0},{4,5},{5,6},{6,7},{7,4},{8,9},{9,10},{10,1... | collective-permute-start | bytes 393224 | tf_op jit(solution)/shard_map/ppermute | solution.py:561
  55.2 7.9 %collective-permute-start.7 = (bf16[512,128]{1,0:T(8,128)(2,1)S(1)}, bf16[512,128]{1,0:T(8,128)(2,1)S(1)}, u32[]{:S(2)}, u32[]{:S(2)}) collective-permute-start(bf16[512,128]{1,0:T(8,128)(2,1)S(1)} %bitcast.6), channel_id=1, source_target_pairs={{0,2},{1,3},{2,0},{3,1},{4,6},{5,7},{6,4},{7,5},{8,10},{9,11},{10,... | collective-permute-start | bytes 393224 | tf_op jit(solution)/shard_map/ppermute | solution.py:561
  57.5 6.3 %collective-permute-start.6 = (bf16[512,128]{1,0:T(8,128)(2,1)S(1)}, bf16[512,128]{1,0:T(8,128)(2,1)S(1)}, u32[]{:S(2)}, u32[]{:S(2)}) collective-permute-start(bf16[512,128]{1,0:T(8,128)(2,1)S(1)} %bitcast.7), channel_id=1, source_target_pairs={{0,3},{1,0},{2,1},{3,2},{4,7},{5,4},{6,5},{7,6},{8,11},{9,8},{10,9... | collective-permute-start | bytes 393224 | tf_op jit(solution)/shard_map/ppermute | solution.py:561
  77.1 1.3 %collective-permute-start.9 = (f32[96,128]{1,0:T(8,128)S(1)}, f32[96,128]{1,0:T(8,128)S(1)}, u32[]{:S(2)}, u32[]{:S(2)}) collective-permute-start(f32[96,128]{1,0:T(8,128)S(1)} %get-tuple-element.38), channel_id=1, source_target_pairs={{0,4},{4,0},{1,5},{5,1},{2,6},{6,2},{3,7},{7,3},{8,12},{12,8},{9,1... | collective-permute-start | bytes 147464 | tf_op jit(solution)/shard_map/ppermute | solution.py:545
  78.4 5.1 %collective-permute-start.12 = (f32[96,128]{1,0:T(8,128)S(1)}, f32[96,128]{1,0:T(8,128)S(1)}, u32[]{:S(2)}, u32[]{:S(2)}) collective-permute-start(f32[96,128]{1,0:T(8,128)S(1)} %add.24), channel_id=1, source_target_pairs={{0,24},{8,16},{16,8},{24,0},{32,56},{40,48},{48,40},{56,32},{1,25}... | collective-permute-start | bytes 147464 | tf_op jit(solution)/shard_map/ppermute | solution.py:545
  79.7 5.9 %collective-permute-start.11 = (f32[96,128]{1,0:T(8,128)S(1)}, f32[96,128]{1,0:T(8,128)S(1)}, u32[]{:S(2)}, u32[]{:S(2)}) collective-permute-start(f32[96,128]{1,0:T(8,128)S(1)} %add.24), channel_id=1, source_target_pairs={{0,16},{8,24},{16,0},{24,8},{32,48},{40,56},{48,32},{56,40},{1,17}... | collective-permute-start | bytes 147464 | tf_op jit(solution)/shard_map/ppermute | solution.py:545
  82.3 4.1 %collective-permute-start.10 = (f32[96,128]{1,0:T(8,128)S(1)}, f32[96,128]{1,0:T(8,128)S(1)}, u32[]{:S(2)}, u32[]{:S(2)}) collective-permute-start(f32[96,128]{1,0:T(8,128)S(1)} %add.24), channel_id=1, source_target_pairs={{0,8},{8,0},{16,24},{24,16},{32,40},{40,32},{48,56},{56,48},{1,9},... | collective-permute-start | bytes 147464 | tf_op jit(solution)/shard_map/ppermute | solution.py:545
  86.4 8.4 %collective-permute-start.13 = (f32[96,128]{1,0:T(8,128)S(1)}, f32[96,128]{1,0:T(8,128)S(1)}, u32[]{:S(2)}, u32[]{:S(2)}) collective-permute-start(f32[96,128]{1,0:T(8,128)S(1)} %add_add_fusion.1), channel_id=1, source_target_pairs={{0,32},{8,40},{16,48},{24,56},{32,0},{40,8},{48,16},{56,24},{1,33}... | collective-permute-start | bytes 147464 | tf_op jit(solution)/shard_map/ppermute | solution.py:545
  94.8 5.4 %collective-permute-start.16 = (f32[96,128]{1,0:T(8,128)S(1)}, f32[96,128]{1,0:T(8,128)S(1)}, u32[]{:S(2)}, u32[]{:S(2)}) collective-permute-start(f32[96,128]{1,0:T(8,128)S(1)} %add.28), channel_id=1, source_target_pairs={{0,192},{64,128},{128,64},{192,0},{1,193},{65,129},{129,65},{193,1... | collective-permute-start | bytes 147464 | tf_op jit(solution)/shard_map/ppermute | solution.py:545
  98.0 5.6 %collective-permute-start.15 = (f32[96,128]{1,0:T(8,128)S(1)}, f32[96,128]{1,0:T(8,128)S(1)}, u32[]{:S(2)}, u32[]{:S(2)}) collective-permute-start(f32[96,128]{1,0:T(8,128)S(1)} %add.28), channel_id=1, source_target_pairs={{0,128},{64,192},{128,0},{192,64},{1,129},{65,193},{129,1},{193,65... | collective-permute-start | bytes 147464 | tf_op jit(solution)/shard_map/ppermute | solution.py:545
  98.6 5.0 %collective-permute-start.14 = (f32[96,128]{1,0:T(8,128)S(1)}, f32[96,128]{1,0:T(8,128)S(1)}, u32[]{:S(2)}, u32[]{:S(2)}) collective-permute-start(f32[96,128]{1,0:T(8,128)S(1)} %add.28), channel_id=1, source_target_pairs={{0,64},{64,0},{128,192},{192,128},{1,65},{65,1},{129,193},{193,129... | collective-permute-start | bytes 147464 | tf_op jit(solution)/shard_map/ppermute | solution.py:545
where the time goes:
time: 124 us
  Pallas kernels  40.7 us (33%)
  starting transfers between devices  40.5 us (33%)
  waiting for transfers between devices  30.9 us (25%)
  blocking collectives  9.7 us (8%)
    ppermute x8, waiting for transfers between devices, swap(): return lax.ppermute(value, axis, [(i, i ^ bit) for i in range(size)])  14.9 us
    pallas_call x1, Pallas kernels, analyse(): pl.pallas_call(analyse_kernel, out_shape=(jax.ShapeDtypeStruct((orders, 4...  13.3 us
    ppermute x8, starting transfers between devices, swap(): return lax.ppermute(value, axis, [(i, i ^ bit) for i in range(size)])  11.6 us
    all_to_all x1, starting transfers between devices, shards(): lax.all_to_all(fields, MA, split_axis=0, concat_axis=0, tiled=True)  11.3 us
    all_to_all x1, blocking collectives, shards(): lax.all_to_all(summed, 'vert', split_axis=0, concat_axis=0, tiled=True)  9.7 us
    pallas_call x1, Pallas kernels, factors(): pl.pallas_call(factors_kernel, out_shape=(jax.ShapeDtypeStruct((n, 4 * n)...  7.89 us
    pallas_call x1, Pallas kernels, synthesize(): pl.pallas_call(synthesize_kernel, out_shape=(jax.ShapeDtypeStruct((cycles...  6.46 us
    all_to_all x1, starting transfers between devices, shards(): lax.all_to_all(returned.reshape(live, orders, columns), MA, split_axis=0,...  5.88 us
  transfers between devices with their start and end apart: 19, of which 12 were waited for; matrix products, arithmetic and copies ran while one was open for 0% of the time, Pallas kernels for 9%

commit v1 on v0

--- a/solution.py
+++ b/solution.py
@@ -192,13 +192,9 @@
     return sine, cosine
 
 
-def transform_kernel(
-    where, begins, counts, weights, slots, received, returned, cosine, sines
-):
+def tables_kernel(slots, cosine, sines):
     orders, longitudes = cosine.shape
     lanes = slots.shape[1]
-    columns = received.shape[1]
-    part = columns // 4
     scale = 1.0 / math.sqrt(orders)
     near = lax.broadcasted_iota(jnp.int32, (lanes, lanes), 1)
     for g in range(slots.shape[0]):
@@ -213,6 +209,24 @@
             sines[span, b * lanes : (b + 1) * lanes] = s.astype(BF16)
             s, c = s * step_c + c * step_s, c * step_c - s * step_s
 
+
+def fourier_tables(slots):
+    table = jax.ShapeDtypeStruct((slots.size, 2 * slots.size), BF16)
+    return pl.pallas_call(
+        tables_kernel,
+        out_shape=(table, table),
+        compiler_params=pltpu.CompilerParams(vmem_limit_bytes=16 << 20),
+        cost_estimate=pl.CostEstimate(
+            flops=10_000_000, bytes_accessed=2 << 20, transcendentals=0
+        ),
+        name="tables",
+    )(slots)
+
+
+def transform_kernel(where, begins, counts, weights, cosine, sines, received, returned):
+    longitudes = cosine.shape[1]
+    columns = received.shape[1]
+    part = columns // 4
     home = (lax.axis_index("ma_0") * 8 + lax.axis_index("ma_1")) * 2 + lax.axis_index("ma_2")
     r = where[0] + where[1] + home
     j = lax.broadcasted_iota(jnp.int32, (1, longitudes), 1)
@@ -232,22 +246,20 @@
     returned[...] = back.astype(BF16)
 
 
-def cycle_transform(where, begins, counts, weights, slots, received):
+def cycle_transform(where, begins, counts, weights, cosine, sines, received):
     vmem = pl.BlockSpec(memory_space=pltpu.VMEM)
     smem = pl.BlockSpec(memory_space=pltpu.SMEM)
-    orders = slots.size
     return pl.pallas_call(
         transform_kernel,
         out_shape=jax.ShapeDtypeStruct(received.shape, BF16),
-        in_specs=[smem] * 4 + [vmem] * 2,
+        in_specs=[smem] * 4 + [vmem] * 3,
         out_specs=vmem,
-        scratch_shapes=[pltpu.VMEM((orders, 2 * orders), BF16)] * 2,
         compiler_params=pltpu.CompilerParams(vmem_limit_bytes=40 << 20),
         cost_estimate=pl.CostEstimate(
             flops=600_000_000, bytes_accessed=3 << 20, transcendentals=0
         ),
         name="transform",
-    )(where, begins, counts, weights, slots, received)
+    )(where, begins, counts, weights, cosine, sines, received)
 
 
 def trial_gram_kernel(
@@ -297,100 +309,160 @@
     )(in_hbm(trial), *received)
 
 
-def analyse_kernel(
-    where, got0, got1, got2, got3, rows0, rows1, rows2, rows3, legendre,
-    tt, applied, gram,
-    got_v, rows_v, wide, adj, leg_v, tt_v, sem_g, sem_r, sem_l, sem_t,
+def placed_pair(adj, x, base, shift, sign0, sign1):
+    cycles, columns = x.shape
+    adj[pl.ds(base + shift, cycles), :] = x * sign0
+    adj[pl.ds(base + WINDOW + shift, cycles), :] = pltpu.roll(x, columns // 2, 1) * sign1
+
+
+def adjoint_signs(columns, vectors):
+    lane = lax.broadcasted_iota(jnp.int32, (1, columns), 1) // vectors
+    one = jnp.ones((1, columns), F32)
+    return jnp.where(lane < 2, one, -one), jnp.where((lane == 0) | (lane == 3), -one, one)
+
+
+ROWS_OF = {0: 0, 1: 1, 3: 2, 2: 3}
+
+
+def analyse_own_kernel(
+    where, got, legendre, tt, own, gram, leg_v, tt_v, wide, adj, sem_l, sem_t
 ):
-    orders, _, vectors, _ = tt.shape
+    orders, _, vectors, degrees = tt.shape
     columns = 4 * vectors
     start = pl.multiple_of(where[0], 16)
     shift = where[1]
-
-    def trial_copy(n):
-        return pltpu.make_async_copy(tt.at[n], tt_v.at[n], sem_t.at[n])
-
+    for n in range(orders):
+        window_copy(legendre, leg_v, sem_l, n, n, start).start()
+        pltpu.make_async_copy(tt.at[n], tt_v.at[n], sem_t.at[n]).start()
+    wide[...] = got[...].astype(F32)
+    adj[...] = jnp.zeros_like(adj)
+    sign0, sign1 = adjoint_signs(columns, vectors)
+    cycles = got.shape[0] // orders
+    total = 0.0
+    for n in range(orders):
+        x = wide[pl.ds(n, cycles, stride=orders), :]
+        base = n % 2 * 2 * WINDOW
+        placed_pair(adj, x, base, shift, sign0, sign1)
+        a = adj[base : base + 2 * WINDOW].T.astype(BF16)
+        window_copy(legendre, leg_v, sem_l, n, n, start).wait()
+        rows = dot(a, leg_v[n].reshape(2 * WINDOW, degrees)).astype(BF16)
+        pltpu.make_async_copy(tt.at[n], tt_v.at[n], sem_t.at[n]).wait()
+        for c in range(4):
+            mine = rows[ROWS_OF[c] * vectors : (ROWS_OF[c] + 1) * vectors]
+            own[n, c] = mine
+            total = total + dot(mine, jnp.concatenate([tt_v[n, c], mine], axis=0), NT)
+    gram[...] = total
+
+
+def analyse_own(where, got, legendre, tt):
+    orders, _, vectors, degrees = tt.shape
+    rows, columns = got.shape
+    vmem = pl.BlockSpec(memory_space=pltpu.VMEM)
+    hbm = pl.BlockSpec(memory_space=pltpu.HBM)
+    block = jax.ShapeDtypeStruct(tt.shape, BF16)
+    return pl.pallas_call(
+        analyse_own_kernel,
+        out_shape=(
+            block,
+            jax.ShapeDtypeStruct((vectors, 2 * vectors), F32),
+            jax.ShapeDtypeStruct((orders, 2, WINDOW, degrees), BF16),
+            block,
+        ),
+        in_specs=[pl.BlockSpec(memory_space=pltpu.SMEM), vmem, hbm, hbm],
+        out_specs=(vmem,) * 4,
+        scratch_shapes=[
+            pltpu.VMEM((rows, columns), F32),
+            pltpu.VMEM((2 * 2 * WINDOW, columns), F32),
+            pltpu.SemaphoreType.DMA((orders,)),
+            pltpu.SemaphoreType.DMA((orders,)),
+        ],
+        compiler_params=pltpu.CompilerParams(vmem_limit_bytes=24 << 20),
+        cost_estimate=pl.CostEstimate(
+            flops=500_000_000, bytes_accessed=5 << 20, transcendentals=0
+        ),
+        name="analyse_own",
+    )(where, got, in_hbm(legendre), in_hbm(tt))
+
+
+def analyse_kernel(
+    where, got1, got2, got3, rows0, rows1, rows2, rows3, own, own_gram, leg_v, tt_v,
+    rest, kept, sent, gram, got_v, rows_v, wide, adj, sem_g, sem_r,
+):
+    orders, _, vectors, degrees = own.shape
+    columns = 4 * vectors
+    shift = where[1]
     got_copies = [
         pltpu.make_async_copy(got, got_v.at[e], sem_g.at[e])
-        for e, got in enumerate((got0, got1, got2, got3))
+        for e, got in enumerate((got1, got2, got3))
     ]
     row_copies = [
         pltpu.make_async_copy(rows, rows_v.at[e], sem_r.at[e])
         for e, rows in enumerate((rows0, rows1, rows2, rows3))
     ]
-    for copy in got_copies:
+    for copy in got_copies + row_copies:
         copy.start()
-    for n in range(orders):
-        window_copy(legendre, leg_v, sem_l, n, n, start).start()
-        trial_copy(n).start()
-    for copy in row_copies:
-        copy.start()
+    adj[...] = jnp.zeros_like(adj)
     for e, copy in enumerate(got_copies):
         copy.wait()
         wide[e] = got_v[e].astype(F32)
-    adj[...] = jnp.zeros_like(adj)
-    lane = lax.broadcasted_iota(jnp.int32, (1, columns), 1) // vectors
-    one = jnp.ones((1, columns), F32)
-    sign0 = jnp.where(lane < 2, one, -one)
-    sign1 = jnp.where((lane == 0) | (lane == 3), -one, one)
-    cycles = got0.shape[0] // orders
-    block = {0: 0, 1: 1, 3: 2, 2: 3}
+    sign0, sign1 = adjoint_signs(columns, vectors)
+    cycles = got1.shape[0] // orders
     total = 0.0
     for n in range(orders):
-        for e in range(4):
+        for e in range(3):
             x = wide[e, pl.ds(n, cycles, stride=orders), :]
-            base = e * 2 * WINDOW + shift
-            adj[pl.ds(base, cycles), :] = x * sign0
-            adj[pl.ds(base + WINDOW, cycles), :] = pltpu.roll(x, columns // 2, 1) * sign1
+            placed_pair(adj, x, e * 2 * WINDOW, shift, sign0, sign1)
         a = jnp.concatenate(
-            [adj[e * 2 * WINDOW : (e + 1) * 2 * WINDOW].T for e in range(4)], axis=0
+            [adj[e * 2 * WINDOW : (e + 1) * 2 * WINDOW].T for e in range(3)], axis=0
         ).astype(BF16)
-        window_copy(legendre, leg_v, sem_l, n, n, start).wait()
-        rows = dot(a, leg_v[n].reshape(2 * WINDOW, leg_v.shape[3])).astype(BF16)
-        trial_copy(n).wait()
+        rows = dot(a, leg_v[n].reshape(2 * WINDOW, degrees)).astype(BF16)
         for c in range(4):
-            b = block[c] * vectors
-            own = [rows[e * columns + b : e * columns + b + vectors] for e in range(4)]
-            every = jnp.concatenate(own, axis=0)
-            applied[n, c] = every
-            total = total + dot(every, jnp.concatenate([tt_v[n, c], own[0]], axis=0), NT)
+            b = ROWS_OF[c] * vectors
+            others = jnp.concatenate(
+                [rows[e * columns + b : e * columns + b + vectors] for e in range(3)], axis=0
+            )
+            rest[n, c] = others
+            total = total + dot(
+                others, jnp.concatenate([tt_v[n, c], own[n, c]], axis=0), NT
+            )
     for copy in row_copies:
         copy.wait()
     gram[:vectors] = (rows_v[0] + rows_v[1]) + (rows_v[2] + rows_v[3])
-    gram[vectors:] = total.T
-
-
-def analyse(where, gots, trial_rows, legendre, tt):
-    orders, _, vectors, degrees = tt.shape
+    gram[vectors:] = jnp.concatenate([own_gram[...], total], axis=0).T
+    half = kept.shape[0]
+    core = lax.axis_index("ma_2")
+    kept[...] = gram[pl.ds(pl.multiple_of(core * half, half), half), :]
+    sent[...] = gram[pl.ds(pl.multiple_of((1 - core) * half, half), half), :]
+
+
+def analyse(where, gots, trial_rows, own, own_gram, leg_v, tt_v):
+    orders, _, vectors, degrees = own.shape
     cycles_rows, columns = gots[0].shape
     vmem = pl.BlockSpec(memory_space=pltpu.VMEM)
     hbm = pl.BlockSpec(memory_space=pltpu.HBM)
     return pl.pallas_call(
         analyse_kernel,
         out_shape=(
-            jax.ShapeDtypeStruct((orders, 4, 4 * vectors, degrees), BF16),
-            jax.ShapeDtypeStruct((3 * vectors, 4 * vectors), F32),
-        ),
-        in_specs=[pl.BlockSpec(memory_space=pltpu.SMEM)] + [hbm] * 10,
-        out_specs=(vmem, vmem),
+            jax.ShapeDtypeStruct((orders, 4, 3 * vectors, degrees), BF16),
+            *([jax.ShapeDtypeStruct((3 * vectors // 2, columns), F32)] * 2),
+        ),
+        in_specs=[pl.BlockSpec(memory_space=pltpu.SMEM)] + [hbm] * 7 + [vmem] * 4,
+        out_specs=(vmem, vmem, vmem),
         scratch_shapes=[
-            pltpu.VMEM((4, cycles_rows, columns), BF16),
+            pltpu.VMEM((3 * vectors, columns), F32),
+            pltpu.VMEM((3, cycles_rows, columns), BF16),
             pltpu.VMEM((4, vectors, columns), F32),
-            pltpu.VMEM((4, cycles_rows, columns), F32),
-            pltpu.VMEM((4 * 2 * WINDOW, columns), F32),
-            pltpu.VMEM((orders, 2, WINDOW, degrees), BF16),
-            pltpu.VMEM((orders, 4, vectors, degrees), BF16),
+            pltpu.VMEM((3, cycles_rows, columns), F32),
+            pltpu.VMEM((3 * 2 * WINDOW, columns), F32),
+            pltpu.SemaphoreType.DMA((3,)),
             pltpu.SemaphoreType.DMA((4,)),
-            pltpu.SemaphoreType.DMA((4,)),
-            pltpu.SemaphoreType.DMA((orders,)),
-            pltpu.SemaphoreType.DMA((orders,)),
         ],
-        compiler_params=pltpu.CompilerParams(vmem_limit_bytes=40 << 20),
-        cost_estimate=pl.CostEstimate(
-            flops=2_000_000_000, bytes_accessed=14 << 20, transcendentals=0
+        compiler_params=pltpu.CompilerParams(vmem_limit_bytes=32 << 20),
+        cost_estimate=pl.CostEstimate(
+            flops=1_500_000_000, bytes_accessed=12 << 20, transcendentals=0
         ),
         name="analyse",
-    )(where, *gots, *trial_rows, in_hbm(legendre), in_hbm(tt))
+    )(where, *gots, *trial_rows, own, own_gram, leg_v, tt_v)
 
 
 def eliminate(work, n):
@@ -451,8 +523,9 @@
     n = cross.shape[0]
     vectors = n // 4
     copies = [
-        pltpu.make_async_copy(grams.at[group], gram_v.at[group], sem.at[group])
-        for group in range(grams.shape[0])
+        pltpu.make_async_copy(grams.at[half, group], gram_v.at[half, group], sem.at[half, group])
+        for group in range(4)
+        for half in range(2)
     ]
     for copy in copies:
         copy.start()
@@ -463,9 +536,11 @@
     ).astype(F32)
     work[0, :, n:] = unit
     work[1, :, n:] = unit
-    for group, copy in enumerate(copies):
-        copy.wait()
-        rows = gram_v[group] * (1.0 / COEFFICIENTS)
+    for group in range(4):
+        copies[2 * group].wait()
+        copies[2 * group + 1].wait()
+        rows = jnp.concatenate([gram_v[0, group], gram_v[1, group]], axis=0)
+        rows = rows * (1.0 / COEFFICIENTS)
         if group:
             rows = pltpu.roll(rows, group * vectors, 1)
         span = pl.ds(group * vectors, vectors)
@@ -487,7 +562,7 @@
 
 
 def factors(grams):
-    _, rows, n = grams.shape
+    _, _, rows, n = grams.shape
     vmem = pl.BlockSpec(memory_space=pltpu.VMEM)
     return pl.pallas_call(
         factors_kernel,
@@ -498,10 +573,10 @@
         in_specs=[pl.BlockSpec(memory_space=pltpu.HBM)],
         out_specs=(vmem, vmem),
         scratch_shapes=[
-            pltpu.VMEM((4, rows, n), F32),
+            pltpu.VMEM((2, 4, rows, n), F32),
             pltpu.VMEM((2, n, 2 * n), F32),
             pltpu.VMEM((n, n), F32),
-            pltpu.SemaphoreType.DMA((4,)),
+            pltpu.SemaphoreType.DMA((2, 4)),
         ],
         compiler_params=pltpu.CompilerParams(vmem_limit_bytes=16 << 20),
         cost_estimate=pl.CostEstimate(
@@ -511,26 +586,27 @@
     )(grams)
 
 
-def mix_kernel(weights, applied, new_basis, out_v, sem):
-    orders, parts, n, degrees = applied.shape
-    for s in range(orders):
-        y = dot(weights[...], applied[s].reshape(parts * n, degrees)).astype(BF16)
-        out_v[s] = y.reshape(n // 4, 4, degrees)
+def mix_kernel(weights, own, rest, new_basis, out_v, sem):
+    orders, parts, vectors, degrees = own.shape
+    for s in range(orders):
+        every = [piece for c in range(parts) for piece in (own[s, c], rest[s, c])]
+        y = dot(weights[...], jnp.concatenate(every, axis=0)).astype(BF16)
+        out_v[s] = y.reshape(vectors, 4, degrees)
         pltpu.make_async_copy(out_v.at[s], new_basis.at[:, s], sem.at[s]).start()
     for s in range(orders):
         pltpu.make_async_copy(out_v.at[s], new_basis.at[:, s], sem.at[s]).wait()
 
 
-def mix(weights, applied):
-    orders, _, n, degrees = applied.shape
+def mix(weights, own, rest):
+    orders, _, vectors, degrees = own.shape
     vmem = pl.BlockSpec(memory_space=pltpu.VMEM)
     return pl.pallas_call(
         mix_kernel,
-        out_shape=pltpu.HBM((n // 4, orders, 4, degrees), BF16),
-        in_specs=[vmem, vmem],
+        out_shape=pltpu.HBM((vectors, orders, 4, degrees), BF16),
+        in_specs=[vmem, vmem, vmem],
         out_specs=pl.BlockSpec(memory_space=pltpu.HBM),
         scratch_shapes=[
-            pltpu.VMEM((orders, n // 4, 4, degrees), BF16),
+            pltpu.VMEM((orders, vectors, 4, degrees), BF16),
             pltpu.SemaphoreType.DMA((orders,)),
         ],
         compiler_params=pltpu.CompilerParams(vmem_limit_bytes=32 << 20),
@@ -538,7 +614,7 @@
             flops=1_100_000_000, bytes_accessed=10 << 20, transcendentals=0
         ),
         name="mix",
-    )(weights, applied)
+    )(weights, own, rest)
 
 
 def swap(value, axis, size, bit):
@@ -550,8 +626,8 @@
     return (value + one) + (two + three)
 
 
-def sum_over_ma(value):
-    value = value + swap(value, "ma_2", 2, 1)
+def sum_over_ma(kept, sent):
+    value = kept + swap(sent, "ma_2", 2, 1)
     value = sum_of_four(value, "ma_1", 8)
     value = value + swap(value, "ma_1", 8, 4)
     return sum_of_four(value, "ma_0", 4)
@@ -572,9 +648,10 @@
     blocks = [lax.ppermute(x, "vert", ring(4, d)) for d, x in enumerate(sent, 1)]
     received = lax.all_to_all(fields, MA, split_axis=0, concat_axis=0, tiled=True)
     tt = arrange(trial_block)
-    received, tt = lax.optimization_barrier((received, tt))
+    cosine, sines = fourier_tables(order_slot.reshape(-1, 128))
+    received, tt, cosine, sines = lax.optimization_barrier((received, tt, cosine, sines))
     returned = cycle_transform(
-        where, cycle_start, cycle_count, cycle_weight, order_slot.reshape(-1, 128),
+        where, cycle_start, cycle_count, cycle_weight, cosine, sines,
         received.reshape(live * orders, columns),
     )
     order_fields = lax.all_to_all(
@@ -586,11 +663,12 @@
     ]
     order_fields, *trial_rows = lax.optimization_barrier((order_fields, *trial_rows))
     gots = from_groups(order_fields.reshape(live * orders, columns))
-    applied, gram = analyse(where, gots, trial_rows, legendre, tt)
-    summed = jnp.broadcast_to(sum_over_ma(gram)[None], (4, *gram.shape))
-    grams = lax.all_to_all(summed, "vert", split_axis=0, concat_axis=0, tiled=True)
-    weights, ritz_matrix = factors(grams)
-    return (mix(weights, applied), ritz_matrix)
+    own, *of_own = analyse_own(where, gots[0], legendre, tt)
+    rest, kept, sent = analyse(where, gots[1:], trial_rows, own, *of_own)
+    summed = jnp.broadcast_to(sum_over_ma(kept, sent)[None], (8, *kept.shape))
+    grams = lax.all_to_all(summed, ("ma_2", "vert"), split_axis=0, concat_axis=0, tiled=True)
+    weights, ritz_matrix = factors(grams.reshape(2, 4, *kept.shape))
+    return (mix(weights, own, rest), ritz_matrix)
 
 
 def solution(mesh):

time: 124 us -> 119 us (0.960)
  the two profiles are of different devices: /device:TPU:64 before, /device:TPU:1 now
where the time goes in v1:
time: 119 us
  starting transfers between devices  42.7 us (36%)
  Pallas kernels  41.3 us (35%)
  waiting for transfers between devices  19.1 us (16%)
  blocking collectives  14.2 us (12%)
    all_to_all x1, blocking collectives, shards(): lax.all_to_all(summed, ('ma_2', 'vert'), split_axis=0, concat_axis=0, til...  14.2 us
    all_to_all x1, starting transfers between devices, shards(): lax.all_to_all(fields, MA, split_axis=0, concat_axis=0, tiled=True)  13.2 us
    ppermute x8, starting transfers between devices, swap(): return lax.ppermute(value, axis, [(i, i ^ bit) for i in range(size)])  13 us
    ppermute x8, waiting for transfers between devices, swap(): return lax.ppermute(value, axis, [(i, i ^ bit) for i in range(size)])  10.7 us
    pallas_call x1, Pallas kernels, factors(): pl.pallas_call(factors_kernel, out_shape=(jax.ShapeDtypeStruct((n, 4 * n)...  7.93 us
    pallas_call x1, Pallas kernels, analyse_own(): pl.pallas_call(analyse_own_kernel, out_shape=(block, jax.ShapeDtypeStruct...  6.79 us
    pallas_call x1, Pallas kernels, synthesize(): pl.pallas_call(synthesize_kernel, out_shape=(jax.ShapeDtypeStruct((cycles...  6.46 us
    ppermute x3, starting transfers between devices, shards(): lax.ppermute(x, 'vert', ring(4, d))  5.72 us
  transfers between devices with their start and end apart: 19, of which 9 were waited for; matrix products, arithmetic and copies ran while one was open for 0% of the time, Pallas kernels for 16%

profile of v1, /device:TPU:1, one launch (start us, length us, event | category | flops | bytes accessed | tf_op | source)
XLA Modules:
  0.0 119.1 jit_solution(13910009460559984100)
XLA Ops:
  0.6 0.7 copy-done
  1.3 6.5 %synthesize.1 = (bf16[64,8,128]{2,1,0:T(8,128)(2,1)}, bf16[2,32,4,1024]{3,2,1,0:T(4,128)(2,1)}, bf16[2,32,4,1024]{3,2,1,0:T(4,128)(2,1)}, bf16[2,32,4,1024]{3,2,1,0:T(4,128)(2,1)}, s32[2]{0:T(128)S(1)}) custom-call(s32[2,128]{1,0:T(2,128)S(1)} %bitcast.12, bf16[32,8,4,1024]{3,2,1,0:T(4,128)(2,1)} %trial.5, bf16[8,2,256,1024]{3,2,1,0:T(8,128)(2,1)} %legendre.3), custom_call_target="tpu_custom_call" | custom-call | flops 600000000 | bytes 5242880 | tf_op jit(solution)/shard_map/synthesize/pallas_call | solution.py:108
  7.8 2.1 %collective-permute-start = (bf16[2,32,4,1024]{3,2,1,0:T(4,128)(2,1)}, bf16[2,32,4,1024]{3,2,1,0:T(4,128)(2,1)S(1)}, u32[]{:S(2)}, u32[]{:S(2)}) collective-permute-start(bf16[2,32,4,1024]{3,2,1,0:T(4,128)(2,1)} %get-tuple-element.38), channel_id=1, source_target_pairs={{0,1},{1,2},{2,3},{3,0},{4,5},{5,6},{6,7},{7,4},{8,9},{9,10},{10,1... | collective-permute-start | bytes 1572872 | tf_op jit(solution)/shard_map/ppermute | solution.py:648
  9.9 2.5 %collective-permute-start.1 = (bf16[2,32,4,1024]{3,2,1,0:T(4,128)(2,1)}, bf16[2,32,4,1024]{3,2,1,0:T(4,128)(2,1)S(1)}, u32[]{:S(2)}, u32[]{:S(2)}) collective-permute-start(bf16[2,32,4,1024]{3,2,1,0:T(4,128)(2,1)} %get-tuple-element.39), channel_id=1, source_target_pairs={{0,2},{1,3},{2,0},{3,1},{4,6},{5,7},{6,4},{7,5},{8,10},{9,11},{10,... | collective-permute-start | bytes 1572872 | tf_op jit(solution)/shard_map/ppermute | solution.py:648
  12.4 1.1 collective-permute-start.2
  13.5 13.2 %all-to-all-start = ((bf16[64,8,128]{2,1,0:T(8,128)(2,1)}), bf16[64,8,128]{2,1,0:T(8,128)(2,1)S(1)}, u32[]{:S(2)}, u32[]{:S(2)}) async-start(bf16[64,8,128]{2,1,0:T(8,128)(2,1)} %get-tuple-element.32), calls=%async_computation | async-start | bytes 262144 | tf_op jit(solution)/shard_map/all_to_all | solution.py:649
  26.7 2.1 %tables.1 = (bf16[512,1024]{1,0:T(8,128)(2,1)S(1)}, bf16[512,1024]{1,0:T(8,128)(2,1)S(1)}) custom-call(s32[4,128]{1,0:T(4,128)S(1)} %bitcast.13), custom_call_target="tpu_custom_call" | custom-call | flops 10000000 | bytes 2097152 | tf_op jit(solution)/shard_map/tables/pallas_call | solution.py:215
  28.9 3.6 %arrange.1.tt = bf16[8,4,32,1024]{3,2,1,0:T(8,128)(2,1)} custom-call(bf16[32,8,4,1024]{3,2,1,0:T(4,128)(2,1)} %trial.5), custom_call_target="tpu_custom_call" | custom-call | flops 300000000 | bytes 4194304 | tf_op jit(solution)/shard_map/arrange/pallas_call | solution.py:155
  32.4 4.6 %all-to-all-done = bf16[64,8,128]{2,1,0:T(8,128)(2,1)S(1)} async-done(((bf16[64,8,128]{2,1,0:T(8,128)(2,1)}), bf16[64,8,128]{2,1,0:T(8,128)(2,1)S(1)}, u32[]{:S(2)}, u32[]{:S(2)}) %all-to-all-start) | async-done | bytes 131104 | tf_op jit(solution)/shard_map/all_to_all | solution.py:649
  37.1 2.4 %transform.1 = bf16[512,128]{1,0:T(8,128)(2,1)} custom-call(s32[2]{0:T(128)S(1)} %get-tuple-element.31.where, s32[256]{0:T(256)S(1)} %copy-done.2, s32[256]{0:T(256)S(1)} %copy-done.1, f32[256]{0:T(256)S(1)} %copy-done.3, bf16[512,1024]{1,0:T(8,128)(2,1)S(1)} %get-tuple-element.35.cosine, bf16[512,1024]{1,0:T(8,128)(2,1)S(1)} %get-tuple-element.36.sines, ...), custom_call_target="tpu_custom_call" | custom-call | flops 600000000 | bytes 3145728 | tf_op jit(solution)/shard_map/transform/pallas_call | solution.py:252
  39.5 5.7 %all-to-all-start.1 = ((bf16[64,8,128]{2,1,0:T(8,128)(2,1)}), bf16[64,8,128]{2,1,0:T(8,128)(2,1)S(1)}, u32[]{:S(2)}, u32[]{:S(2)}) async-start(bf16[64,8,128]{2,1,0:T(8,128)(2,1)} %bitcast.3), calls=%async_computation.1 | async-start | bytes 262144 | tf_op jit(solution)/shard_map/all_to_all | solution.py:657
  45.2 4.4 %trial_gram.1 = (f32[32,128]{1,0:T(8,128)S(1)}, f32[32,128]{1,0:T(8,128)S(1)}, f32[32,128]{1,0:T(8,128)S(1)}, f32[32,128]{1,0:T(8,128)S(1)}) custom-call(bf16[32,8,4,1024]{3,2,1,0:T(4,128)(2,1)} %trial.5, bf16[2,32,4,1024]{3,2,1,0:T(4,128)(2,1)S(1)} %collective-permute-done.block1, bf16[2,32,4,1024]{3,2,1,0:T(4,128)(2,1)S(1)} %collective-permute-done.1.block2, ...), custom_call_target="tpu_custom_call" | custom-call | flops 600000000 | bytes 2097152 | tf_op jit(solution)/shard_map/trial_gram/pallas_call | solution.py:296
  49.8 2.1 %collective-permute-start.4 = (f32[32,128]{1,0:T(8,128)S(1)}, f32[32,128]{1,0:T(8,128)S(1)}, u32[]{:S(2)}, u32[]{:S(2)}) collective-permute-start(f32[32,128]{1,0:T(8,128)S(1)} %get-tuple-element.43), channel_id=1, source_target_pairs={{0,2},{1,3},{2,0},{3,1},{4,6},{5,7},{6,4},{7,5},{8,10},{9,11},{10,... | collective-permute-start | bytes 49160 | tf_op jit(solution)/shard_map/ppermute | solution.py:662
  51.8 3.7 %all-to-all-done.1 = bf16[64,8,128]{2,1,0:T(8,128)(2,1)S(1)} async-done(((bf16[64,8,128]{2,1,0:T(8,128)(2,1)}), bf16[64,8,128]{2,1,0:T(8,128)(2,1)S(1)}, u32[]{:S(2)}, u32[]{:S(2)}) %all-to-all-start.1) | async-done | bytes 131104 | tf_op jit(solution)/shard_map/all_to_all | solution.py:657
  56.0 1.4 %collective-permute-start.7 = (bf16[512,128]{1,0:T(8,128)(2,1)S(1)}, bf16[512,128]{1,0:T(8,128)(2,1)S(1)}, u32[]{:S(2)}, u32[]{:S(2)}) collective-permute-start(bf16[512,128]{1,0:T(8,128)(2,1)S(1)} %bitcast.7), channel_id=1, source_target_pairs={{0,2},{1,3},{2,0},{3,1},{4,6},{5,7},{6,4},{7,5},{8,10},{9,11},{10,... | collective-permute-start | bytes 393224 | tf_op jit(solution)/shard_map/ppermute | solution.py:637
  57.4 1.1 collective-permute-start.6
  58.5 6.8 %analyse_own.1 = (bf16[8,4,32,1024]{3,2,1,0:T(8,128)(2,1)S(1)}, f32[32,64]{1,0:T(8,128)S(1)}, bf16[8,2,80,1024]{3,2,1,0:T(8,128)(2,1)S(1)}, bf16[8,4,32,1024]{3,2,1,0:T(8,128)(2,1)S(1)}) custom-call(s32[2]{0:T(128)S(1)} %get-tuple-element.31.where, bf16[512,128]{1,0:T(8,128)(2,1)S(1)} %bitcast.9, bf16[8,2,256,1024]{3,2,1,0:T(8,128)(2,1)} %legendre.3, ...), custom_call_target="tpu_custom_call" | custom-call | flops 500000000 | bytes 5242880 | tf_op jit(solution)/shard_map/analyse_own/pallas_call | solution.py:363
  65.3 5.5 %analyse.1 = (bf16[8,4,96,1024]{3,2,1,0:T(8,128)(2,1)S(1)}, f32[48,128]{1,0:T(8,128)S(1)}, f32[48,128]{1,0:T(8,128)S(1)}) custom-call(s32[2]{0:T(128)S(1)} %get-tuple-element.31.where, bf16[512,128]{1,0:T(8,128)(2,1)S(1)} %collective-permute-done.6.got1, bf16[512,128]{1,0:T(8,128)(2,1)S(1)} %collective-permute-done.7.got2, ...), custom_call_target="tpu_custom_call" | custom-call | flops 1500000000 | bytes 12582912 | tf_op jit(solution)/shard_map/analyse/pallas_call | solution.py:443
  70.8 2.7 %collective-permute-start.9 = (f32[48,128]{1,0:T(8,128)S(1)}, f32[48,128]{1,0:T(8,128)S(1)}, u32[]{:S(2)}, u32[]{:S(2)}) collective-permute-start(f32[48,128]{1,0:T(8,128)S(1)} %get-tuple-element.56), channel_id=1, source_target_pairs={{0,4},{4,0},{1,5},{5,1},{2,6},{6,2},{3,7},{7,3},{8,12},{12,8},{9,1... | collective-permute-start | bytes 73736 | tf_op jit(solution)/shard_map/ppermute | solution.py:621
  73.5 0.8 collective-permute-done.9
  74.3 3.1 %collective-permute-start.12 = (f32[48,128]{1,0:T(8,128)S(1)}, f32[48,128]{1,0:T(8,128)S(1)}, u32[]{:S(2)}, u32[]{:S(2)}) collective-permute-start(f32[48,128]{1,0:T(8,128)S(1)} %add.24), channel_id=1, source_target_pairs={{0,24},{8,16},{16,8},{24,0},{32,56},{40,48},{48,40},{56,32},{1,25}... | collective-permute-start | bytes 73736 | tf_op jit(solution)/shard_map/ppermute | solution.py:621
  77.4 0.5 collective-permute-start.10
  77.9 0.9 collective-permute-done.12
  78.8 2.3 %collective-permute-done.11 = f32[48,128]{1,0:T(8,128)S(1)} collective-permute-done((f32[48,128]{1,0:T(8,128)S(1)}, f32[48,128]{1,0:T(8,128)S(1)}, u32[]{:S(2)}, u32[]{:S(2)}) %collective-permute-start.11) | collective-permute-done | bytes 24608 | tf_op jit(solution)/shard_map/ppermute | solution.py:621
  81.1 3.6 %collective-permute-start.13 = (f32[48,128]{1,0:T(8,128)S(1)}, f32[48,128]{1,0:T(8,128)S(1)}, u32[]{:S(2)}, u32[]{:S(2)}) collective-permute-start(f32[48,128]{1,0:T(8,128)S(1)} %add_add_fusion.1), channel_id=1, source_target_pairs={{0,32},{8,40},{16,48},{24,56},{32,0},{40,8},{48,16},{56,24},{1,33}... | collective-permute-start | bytes 73736 | tf_op jit(solution)/shard_map/ppermute | solution.py:621
  84.7 3.1 %collective-permute-done.13 = f32[48,128]{1,0:T(8,128)S(1)} collective-permute-done((f32[48,128]{1,0:T(8,128)S(1)}, f32[48,128]{1,0:T(8,128)S(1)}, u32[]{:S(2)}, u32[]{:S(2)}) %collective-permute-start.13) | collective-permute-done | bytes 24608 | tf_op jit(solution)/shard_map/ppermute | solution.py:621
  87.8 2.5 %collective-permute-start.16 = (f32[48,128]{1,0:T(8,128)S(1)}, f32[48,128]{1,0:T(8,128)S(1)}, u32[]{:S(2)}, u32[]{:S(2)}) collective-permute-start(f32[48,128]{1,0:T(8,128)S(1)} %add.28), channel_id=1, source_target_pairs={{0,192},{64,128},{128,64},{192,0},{1,193},{65,129},{129,65},{193,1... | collective-permute-start | bytes 73736 | tf_op jit(solution)/shard_map/ppermute | solution.py:621
  91.0 0.6 collective-permute-done.16
  91.7 2.8 %collective-permute-done.15 = f32[48,128]{1,0:T(8,128)S(1)} collective-permute-done((f32[48,128]{1,0:T(8,128)S(1)}, f32[48,128]{1,0:T(8,128)S(1)}, u32[]{:S(2)}, u32[]{:S(2)}) %collective-permute-start.15) | collective-permute-done | bytes 24608 | tf_op jit(solution)/shard_map/ppermute | solution.py:621
  94.5 14.2 %all_to_all.15 = f32[8,48,128]{2,1,0:T(8,128)S(1)} all-to-all(f32[8,48,128]{2,1,0:T(8,128)S(1)} %broadcast_in_dim.2), channel_id=1, replica_groups=mesh['ma_0'=4,'ma_1'=8,'ma_2'=2,'vert'=4] {'ma_2','vert'}, dimensions={0} | all-to-all | bytes 393216 | tf_op jit(solution)/shard_map/all_to_all | solution.py:669
  108.8 7.9 %factors.1 = (bf16[128,512]{1,0:T(8,128)(2,1)S(1)}, f32[128,128]{1,0:T(8,128)}) custom-call(f32[2,4,48,128]{3,2,1,0:T(8,128)S(1)} %bitcast.11), custom_call_target="tpu_custom_call" | custom-call | flops 100000000 | bytes 1048576 | tf_op jit(solution)/shard_map/factors/pallas_call | solution.py:567
  116.7 2.2 %mix.1 = bf16[32,8,4,1024]{3,2,1,0:T(4,128)(2,1)} custom-call(bf16[128,512]{1,0:T(8,128)(2,1)S(1)} %get-tuple-element.57.weights, bf16[8,4,32,1024]{3,2,1,0:T(8,128)(2,1)S(1)} %get-tuple-element.51.own, bf16[8,4,96,1024]{3,2,1,0:T(8,128)(2,1)S(1)} %get-tuple-element.58.rest), custom_call_target="tpu_custom_call" | custom-call | flops 1100000000 | bytes 10485760 | tf_op jit(solution)/shard_map/mix/pallas_call | solution.py:603
  (31 shorter events, 1.3 us)
Async XLA Ops:
  0.6 0.7 copy-start
  1.3 25.4 %copy-start.4 = (s32[512]{0:T(512)S(1)}, s32[512]{0:T(512)}, u32[]{:S(2)}) copy-start(s32[512]{0:T(512)} %param.8) | copy-start | bytes 6148
  7.8 37.4 %collective-permute-start = (bf16[2,32,4,1024]{3,2,1,0:T(4,128)(2,1)}, bf16[2,32,4,1024]{3,2,1,0:T(4,128)(2,1)S(1)}, u32[]{:S(2)}, u32[]{:S(2)}) collective-permute-start(bf16[2,32,4,1024]{3,2,1,0:T(4,128)(2,1)} %get-tuple-element.38), channel_id=1, source_target_pairs={{0,1},{1,2},{2,3},{3,0},{4,5},{5,6},{6,7},{7,4},{8,9},{9,10},{10,1... | collective-permute-start | bytes 1572872 | tf_op jit(solution)/shard_map/ppermute | solution.py:648
  9.9 35.3 %collective-permute-start.1 = (bf16[2,32,4,1024]{3,2,1,0:T(4,128)(2,1)}, bf16[2,32,4,1024]{3,2,1,0:T(4,128)(2,1)S(1)}, u32[]{:S(2)}, u32[]{:S(2)}) collective-permute-start(bf16[2,32,4,1024]{3,2,1,0:T(4,128)(2,1)} %get-tuple-element.39), channel_id=1, source_target_pairs={{0,2},{1,3},{2,0},{3,1},{4,6},{5,7},{6,4},{7,5},{8,10},{9,11},{10,... | collective-permute-start | bytes 1572872 | tf_op jit(solution)/shard_map/ppermute | solution.py:648
  12.4 32.9 %collective-permute-start.2 = (bf16[2,32,4,1024]{3,2,1,0:T(4,128)(2,1)}, bf16[2,32,4,1024]{3,2,1,0:T(4,128)(2,1)}, u32[]{:S(2)}, u32[]{:S(2)}) collective-permute-start(bf16[2,32,4,1024]{3,2,1,0:T(4,128)(2,1)} %get-tuple-element.40), channel_id=1, source_target_pairs={{0,3},{1,0},{2,1},{3,2},{4,7},{5,4},{6,5},{7,6},{8,11},{9,8},{10,9... | collective-permute-start | bytes 1572872 | tf_op jit(solution)/shard_map/ppermute | solution.py:648
  13.5 23.5 %all-to-all-start = ((bf16[64,8,128]{2,1,0:T(8,128)(2,1)}), bf16[64,8,128]{2,1,0:T(8,128)(2,1)S(1)}, u32[]{:S(2)}, u32[]{:S(2)}) async-start(bf16[64,8,128]{2,1,0:T(8,128)(2,1)} %get-tuple-element.32), calls=%async_computation | async-start | bytes 262144 | tf_op jit(solution)/shard_map/all_to_all | solution.py:649
  28.8 8.2 %copy-start.1 = (s32[256]{0:T(256)S(1)}, s32[256]{0:T(256)}, u32[]{:S(2)}) copy-start(s32[256]{0:T(256)} %counts.1) | copy-start | bytes 3076
  28.8 8.2 %copy-start.2 = (s32[256]{0:T(256)S(1)}, s32[256]{0:T(256)}, u32[]{:S(2)}) copy-start(s32[256]{0:T(256)} %begins.1) | copy-start | bytes 3076
  28.8 8.2 %copy-start.3 = (f32[256]{0:T(256)S(1)}, f32[256]{0:T(256)}, u32[]{:S(2)}) copy-start(f32[256]{0:T(256)} %weights.1) | copy-start | bytes 3076
  39.5 16.1 %all-to-all-start.1 = ((bf16[64,8,128]{2,1,0:T(8,128)(2,1)}), bf16[64,8,128]{2,1,0:T(8,128)(2,1)S(1)}, u32[]{:S(2)}, u32[]{:S(2)}) async-start(bf16[64,8,128]{2,1,0:T(8,128)(2,1)} %bitcast.3), calls=%async_computation.1 | async-start | bytes 262144 | tf_op jit(solution)/shard_map/all_to_all | solution.py:657
  49.7 5.9 %collective-permute-start.3 = (f32[32,128]{1,0:T(8,128)S(1)}, f32[32,128]{1,0:T(8,128)S(1)}, u32[]{:S(2)}, u32[]{:S(2)}) collective-permute-start(f32[32,128]{1,0:T(8,128)S(1)} %get-tuple-element.42), channel_id=1, source_target_pairs={{0,3},{1,0},{2,1},{3,2},{4,7},{5,4},{6,5},{7,6},{8,11},{9,8},{10,9... | collective-permute-start | bytes 49160 | tf_op jit(solution)/shard_map/ppermute | solution.py:662
  49.8 5.8 %collective-permute-start.4 = (f32[32,128]{1,0:T(8,128)S(1)}, f32[32,128]{1,0:T(8,128)S(1)}, u32[]{:S(2)}, u32[]{:S(2)}) collective-permute-start(f32[32,128]{1,0:T(8,128)S(1)} %get-tuple-element.43), channel_id=1, source_target_pairs={{0,2},{1,3},{2,0},{3,1},{4,6},{5,7},{6,4},{7,5},{8,10},{9,11},{10,... | collective-permute-start | bytes 49160 | tf_op jit(solution)/shard_map/ppermute | solution.py:662
  51.8 3.8 %collective-permute-start.5 = (f32[32,128]{1,0:T(8,128)S(1)}, f32[32,128]{1,0:T(8,128)S(1)}, u32[]{:S(2)}, u32[]{:S(2)}) collective-permute-start(f32[32,128]{1,0:T(8,128)S(1)} %get-tuple-element.44), channel_id=1, source_target_pairs={{0,1},{1,2},{2,3},{3,0},{4,5},{5,6},{6,7},{7,4},{8,9},{9,10},{10,1... | collective-permute-start | bytes 49160 | tf_op jit(solution)/shard_map/ppermute | solution.py:662
  55.6 9.6 %collective-permute-start.8 = (bf16[512,128]{1,0:T(8,128)(2,1)S(1)}, bf16[512,128]{1,0:T(8,128)(2,1)S(1)}, u32[]{:S(2)}, u32[]{:S(2)}) collective-permute-start(bf16[512,128]{1,0:T(8,128)(2,1)S(1)} %bitcast.6), channel_id=1, source_target_pairs={{0,1},{1,2},{2,3},{3,0},{4,5},{5,6},{6,7},{7,4},{8,9},{9,10},{10,1... | collective-permute-start | bytes 393224 | tf_op jit(solution)/shard_map/ppermute | solution.py:637
  56.0 9.3 %collective-permute-start.7 = (bf16[512,128]{1,0:T(8,128)(2,1)S(1)}, bf16[512,128]{1,0:T(8,128)(2,1)S(1)}, u32[]{:S(2)}, u32[]{:S(2)}) collective-permute-start(bf16[512,128]{1,0:T(8,128)(2,1)S(1)} %bitcast.7), channel_id=1, source_target_pairs={{0,2},{1,3},{2,0},{3,1},{4,6},{5,7},{6,4},{7,5},{8,10},{9,11},{10,... | collective-permute-start | bytes 393224 | tf_op jit(solution)/shard_map/ppermute | solution.py:637
  57.4 7.9 %collective-permute-start.6 = (bf16[512,128]{1,0:T(8,128)(2,1)S(1)}, bf16[512,128]{1,0:T(8,128)(2,1)S(1)}, u32[]{:S(2)}, u32[]{:S(2)}) collective-permute-start(bf16[512,128]{1,0:T(8,128)(2,1)S(1)} %bitcast.8), channel_id=1, source_target_pairs={{0,3},{1,0},{2,1},{3,2},{4,7},{5,4},{6,5},{7,6},{8,11},{9,8},{10,9... | collective-permute-start | bytes 393224 | tf_op jit(solution)/shard_map/ppermute | solution.py:637
  70.8 3.5 %collective-permute-start.9 = (f32[48,128]{1,0:T(8,128)S(1)}, f32[48,128]{1,0:T(8,128)S(1)}, u32[]{:S(2)}, u32[]{:S(2)}) collective-permute-start(f32[48,128]{1,0:T(8,128)S(1)} %get-tuple-element.56), channel_id=1, source_target_pairs={{0,4},{4,0},{1,5},{5,1},{2,6},{6,2},{3,7},{7,3},{8,12},{12,8},{9,1... | collective-permute-start | bytes 73736 | tf_op jit(solution)/shard_map/ppermute | solution.py:621
  74.3 4.5 %collective-permute-start.12 = (f32[48,128]{1,0:T(8,128)S(1)}, f32[48,128]{1,0:T(8,128)S(1)}, u32[]{:S(2)}, u32[]{:S(2)}) collective-permute-start(f32[48,128]{1,0:T(8,128)S(1)} %add.24), channel_id=1, source_target_pairs={{0,24},{8,16},{16,8},{24,0},{32,56},{40,48},{48,40},{56,32},{1,25}... | collective-permute-start | bytes 73736 | tf_op jit(solution)/shard_map/ppermute | solution.py:621
  77.4 3.7 %collective-permute-start.11 = (f32[48,128]{1,0:T(8,128)S(1)}, f32[48,128]{1,0:T(8,128)S(1)}, u32[]{:S(2)}, u32[]{:S(2)}) collective-permute-start(f32[48,128]{1,0:T(8,128)S(1)} %add.24), channel_id=1, source_target_pairs={{0,16},{8,24},{16,0},{24,8},{32,48},{40,56},{48,32},{56,40},{1,17}... | collective-permute-start | bytes 73736 | tf_op jit(solution)/shard_map/ppermute | solution.py:621
  77.4 3.7 %collective-permute-start.10 = (f32[48,128]{1,0:T(8,128)S(1)}, f32[48,128]{1,0:T(8,128)S(1)}, u32[]{:S(2)}, u32[]{:S(2)}) collective-permute-start(f32[48,128]{1,0:T(8,128)S(1)} %add.24), channel_id=1, source_target_pairs={{0,8},{8,0},{16,24},{24,16},{32,40},{40,32},{48,56},{56,48},{1,9},... | collective-permute-start | bytes 73736 | tf_op jit(solution)/shard_map/ppermute | solution.py:621
  81.1 6.7 %collective-permute-start.13 = (f32[48,128]{1,0:T(8,128)S(1)}, f32[48,128]{1,0:T(8,128)S(1)}, u32[]{:S(2)}, u32[]{:S(2)}) collective-permute-start(f32[48,128]{1,0:T(8,128)S(1)} %add_add_fusion.1), channel_id=1, source_target_pairs={{0,32},{8,40},{16,48},{24,56},{32,0},{40,8},{48,16},{56,24},{1,33}... | collective-permute-start | bytes 73736 | tf_op jit(solution)/shard_map/ppermute | solution.py:621
  87.8 3.9 %collective-permute-start.16 = (f32[48,128]{1,0:T(8,128)S(1)}, f32[48,128]{1,0:T(8,128)S(1)}, u32[]{:S(2)}, u32[]{:S(2)}) collective-permute-start(f32[48,128]{1,0:T(8,128)S(1)} %add.28), channel_id=1, source_target_pairs={{0,192},{64,128},{128,64},{192,0},{1,193},{65,129},{129,65},{193,1... | collective-permute-start | bytes 73736 | tf_op jit(solution)/shard_map/ppermute | solution.py:621
  90.3 4.2 %collective-permute-start.15 = (f32[48,128]{1,0:T(8,128)S(1)}, f32[48,128]{1,0:T(8,128)S(1)}, u32[]{:S(2)}, u32[]{:S(2)}) collective-permute-start(f32[48,128]{1,0:T(8,128)S(1)} %add.28), channel_id=1, source_target_pairs={{0,128},{64,192},{128,0},{192,64},{1,129},{65,193},{129,1},{193,65... | collective-permute-start | bytes 73736 | tf_op jit(solution)/shard_map/ppermute | solution.py:621
  90.7 3.8 %collective-permute-start.14 = (f32[48,128]{1,0:T(8,128)S(1)}, f32[48,128]{1,0:T(8,128)S(1)}, u32[]{:S(2)}, u32[]{:S(2)}) collective-permute-start(f32[48,128]{1,0:T(8,128)S(1)} %add.28), channel_id=1, source_target_pairs={{0,64},{64,0},{128,192},{192,128},{1,65},{65,1},{129,193},{193,129... | collective-permute-start | bytes 73736 | tf_op jit(solution)/shard_map/ppermute | solution.py:621

commit v2 on v1

--- a/solution.py
+++ b/solution.py
@@ -51,8 +51,10 @@
 
 def synthesize_kernel(
     counts, trial, legendre, fields, sent1, sent2, sent3, where,
-    tr_v, leg_v, one, two, prod, sem_t, sem_l, sem_o,
+    counts_v, tr_v, leg_v, one, two, prod, sem_c, sem_t, sem_l, sem_o,
 ):
+    count_copy = pltpu.make_async_copy(counts, counts_v, sem_c.at[0])
+    count_copy.start()
     vectors, orders = trial.shape[:2]
     me = lax.axis_index("vert")
     pair = orders // 4
@@ -65,7 +67,8 @@
 
     for s in range(orders):
         pltpu.make_async_copy(trial.at[:, s], tr_v.at[s], sem_t.at[s]).start()
-    live = counts[...] > 0
+    count_copy.wait()
+    live = counts_v[...] > 0
     cycle = lax.broadcasted_iota(jnp.int32, live.shape, 0) * live.shape[1]
     cycle = cycle + lax.broadcasted_iota(jnp.int32, live.shape, 1)
     last = legendre.shape[2] - fields.shape[0]
@@ -114,14 +117,16 @@
             sent,
             jax.ShapeDtypeStruct((2,), jnp.int32),
         ),
-        in_specs=[vmem, hbm, hbm],
+        in_specs=[hbm, hbm, hbm],
         out_specs=(vmem, hbm, hbm, hbm, pl.BlockSpec(memory_space=pltpu.SMEM)),
         scratch_shapes=[
+            pltpu.VMEM(counts.shape, jnp.int32),
             pltpu.VMEM((orders, vectors, 4, degrees), BF16),
             pltpu.VMEM((orders, 2, WINDOW, degrees), BF16),
             pltpu.VMEM((2, columns, 128), F32),
             pltpu.VMEM((2, columns, 128), F32),
             pltpu.VMEM((orders * WINDOW, columns), F32),
+            pltpu.SemaphoreType.DMA((1,)),
             pltpu.SemaphoreType.DMA((orders,)),
             pltpu.SemaphoreType.DMA((orders,)),
             pltpu.SemaphoreType.DMA((3,)),
@@ -131,7 +136,7 @@
             flops=600_000_000, bytes_accessed=5 << 20, transcendentals=0
         ),
         name="synthesize",
-    )(counts, in_hbm(trial), in_hbm(legendre))
+    )(in_hbm(counts), in_hbm(trial), in_hbm(legendre))
 
 
 def arrange_kernel(trial, tt, tr_v, tt_v, sem_t, sem_o):

time: 119 us -> 119 us (level)
  transfers between devices with their start and end apart: 19 -> 19, of which waited for: 9 -> 8; matrix products, arithmetic and copies ran while one was open for 0% -> 0% of each run, Pallas kernels for 16% -> 16%
where the time goes in v2:
time: 119 us
  starting transfers between devices  42.6 us (36%)
  Pallas kernels  42.1 us (35%)
  waiting for transfers between devices  19.1 us (16%)
  blocking collectives  14.2 us (12%)
    all_to_all x1, blocking collectives, shards(): lax.all_to_all(summed, ('ma_2', 'vert'), split_axis=0, concat_axis=0, til...  14.2 us
    all_to_all x1, starting transfers between devices, shards(): lax.all_to_all(fields, MA, split_axis=0, concat_axis=0, tiled=True)  13.2 us
    ppermute x8, starting transfers between devices, swap(): return lax.ppermute(value, axis, [(i, i ^ bit) for i in range(size)])  13 us
    ppermute x8, waiting for transfers between devices, swap(): return lax.ppermute(value, axis, [(i, i ^ bit) for i in range(size)])  10.7 us
    pallas_call x1, Pallas kernels, factors(): pl.pallas_call(factors_kernel, out_shape=(jax.ShapeDtypeStruct((n, 4 * n)...  7.93 us
    pallas_call x1, Pallas kernels, synthesize(): pl.pallas_call(synthesize_kernel, out_shape=(jax.ShapeDtypeStruct((cycles...  7.22 us
    pallas_call x1, Pallas kernels, analyse_own(): pl.pallas_call(analyse_own_kernel, out_shape=(block, jax.ShapeDtypeStruct...  6.79 us
    ppermute x3, starting transfers between devices, shards(): lax.ppermute(x, 'vert', ring(4, d))  5.72 us
  transfers between devices with their start and end apart: 19, of which 8 were waited for; matrix products, arithmetic and copies ran while one was open for 0% of the time, Pallas kernels for 16%

profile of v2, /device:TPU:1, one launch (start us, length us, event | category | flops | bytes accessed | tf_op | source)
XLA Modules:
  0.0 119.1 jit_solution(15207373568680507801)
XLA Ops:
  0.6 7.2 %synthesize.1 = (bf16[64,8,128]{2,1,0:T(8,128)(2,1)}, bf16[2,32,4,1024]{3,2,1,0:T(4,128)(2,1)}, bf16[2,32,4,1024]{3,2,1,0:T(4,128)(2,1)}, bf16[2,32,4,1024]{3,2,1,0:T(4,128)(2,1)}, s32[2]{0:T(128)S(1)}) custom-call(s32[2,128]{1,0:T(2,128)} %bitcast.12, bf16[32,8,4,1024]{3,2,1,0:T(4,128)(2,1)} %trial.5, bf16[8,2,256,1024]{3,2,1,0:T(8,128)(2,1)} %legendre.3), custom_call_target="tpu_custom_call" | custom-call | flops 600000000 | bytes 5242880 | tf_op jit(solution)/shard_map/synthesize/pallas_call | solution.py:111
  7.9 2.1 %collective-permute-start = (bf16[2,32,4,1024]{3,2,1,0:T(4,128)(2,1)}, bf16[2,32,4,1024]{3,2,1,0:T(4,128)(2,1)S(1)}, u32[]{:S(2)}, u32[]{:S(2)}) collective-permute-start(bf16[2,32,4,1024]{3,2,1,0:T(4,128)(2,1)} %get-tuple-element.38), channel_id=1, source_target_pairs={{0,1},{1,2},{2,3},{3,0},{4,5},{5,6},{6,7},{7,4},{8,9},{9,10},{10,1... | collective-permute-start | bytes 1572872 | tf_op jit(solution)/shard_map/ppermute | solution.py:653
  10.0 2.5 %collective-permute-start.1 = (bf16[2,32,4,1024]{3,2,1,0:T(4,128)(2,1)}, bf16[2,32,4,1024]{3,2,1,0:T(4,128)(2,1)S(1)}, u32[]{:S(2)}, u32[]{:S(2)}) collective-permute-start(bf16[2,32,4,1024]{3,2,1,0:T(4,128)(2,1)} %get-tuple-element.39), channel_id=1, source_target_pairs={{0,2},{1,3},{2,0},{3,1},{4,6},{5,7},{6,4},{7,5},{8,10},{9,11},{10,... | collective-permute-start | bytes 1572872 | tf_op jit(solution)/shard_map/ppermute | solution.py:653
  12.4 1.1 collective-permute-start.2
  13.6 13.2 %all-to-all-start = ((bf16[64,8,128]{2,1,0:T(8,128)(2,1)}), bf16[64,8,128]{2,1,0:T(8,128)(2,1)S(1)}, u32[]{:S(2)}, u32[]{:S(2)}) async-start(bf16[64,8,128]{2,1,0:T(8,128)(2,1)} %get-tuple-element.32), calls=%async_computation | async-start | bytes 262144 | tf_op jit(solution)/shard_map/all_to_all | solution.py:654
  26.8 2.1 %tables.1 = (bf16[512,1024]{1,0:T(8,128)(2,1)S(1)}, bf16[512,1024]{1,0:T(8,128)(2,1)S(1)}) custom-call(s32[4,128]{1,0:T(4,128)S(1)} %bitcast.13), custom_call_target="tpu_custom_call" | custom-call | flops 10000000 | bytes 2097152 | tf_op jit(solution)/shard_map/tables/pallas_call | solution.py:220
  28.9 3.6 %arrange.1.tt = bf16[8,4,32,1024]{3,2,1,0:T(8,128)(2,1)} custom-call(bf16[32,8,4,1024]{3,2,1,0:T(4,128)(2,1)} %trial.5), custom_call_target="tpu_custom_call" | custom-call | flops 300000000 | bytes 4194304 | tf_op jit(solution)/shard_map/arrange/pallas_call | solution.py:160
  32.5 4.6 %all-to-all-done = bf16[64,8,128]{2,1,0:T(8,128)(2,1)S(1)} async-done(((bf16[64,8,128]{2,1,0:T(8,128)(2,1)}), bf16[64,8,128]{2,1,0:T(8,128)(2,1)S(1)}, u32[]{:S(2)}, u32[]{:S(2)}) %all-to-all-start) | async-done | bytes 131104 | tf_op jit(solution)/shard_map/all_to_all | solution.py:654
  37.1 2.4 %transform.1 = bf16[512,128]{1,0:T(8,128)(2,1)} custom-call(s32[2]{0:T(128)S(1)} %get-tuple-element.31.where, s32[256]{0:T(256)S(1)} %copy-done.1, s32[256]{0:T(256)S(1)} %copy-done, f32[256]{0:T(256)S(1)} %copy-done.2, bf16[512,1024]{1,0:T(8,128)(2,1)S(1)} %get-tuple-element.35.cosine, bf16[512,1024]{1,0:T(8,128)(2,1)S(1)} %get-tuple-element.36.sines, ...), custom_call_target="tpu_custom_call" | custom-call | flops 600000000 | bytes 3145728 | tf_op jit(solution)/shard_map/transform/pallas_call | solution.py:257
  39.6 5.7 %all-to-all-start.1 = ((bf16[64,8,128]{2,1,0:T(8,128)(2,1)}), bf16[64,8,128]{2,1,0:T(8,128)(2,1)S(1)}, u32[]{:S(2)}, u32[]{:S(2)}) async-start(bf16[64,8,128]{2,1,0:T(8,128)(2,1)} %bitcast.3), calls=%async_computation.1 | async-start | bytes 262144 | tf_op jit(solution)/shard_map/all_to_all | solution.py:662
  45.3 4.4 %trial_gram.1 = (f32[32,128]{1,0:T(8,128)S(1)}, f32[32,128]{1,0:T(8,128)S(1)}, f32[32,128]{1,0:T(8,128)S(1)}, f32[32,128]{1,0:T(8,128)S(1)}) custom-call(bf16[32,8,4,1024]{3,2,1,0:T(4,128)(2,1)} %trial.5, bf16[2,32,4,1024]{3,2,1,0:T(4,128)(2,1)S(1)} %collective-permute-done.block1, bf16[2,32,4,1024]{3,2,1,0:T(4,128)(2,1)S(1)} %collective-permute-done.1.block2, ...), custom_call_target="tpu_custom_call" | custom-call | flops 600000000 | bytes 2097152 | tf_op jit(solution)/shard_map/trial_gram/pallas_call | solution.py:301
  49.8 2.1 %collective-permute-start.4 = (f32[32,128]{1,0:T(8,128)S(1)}, f32[32,128]{1,0:T(8,128)S(1)}, u32[]{:S(2)}, u32[]{:S(2)}) collective-permute-start(f32[32,128]{1,0:T(8,128)S(1)} %get-tuple-element.43), channel_id=1, source_target_pairs={{0,2},{1,3},{2,0},{3,1},{4,6},{5,7},{6,4},{7,5},{8,10},{9,11},{10,... | collective-permute-start | bytes 49160 | tf_op jit(solution)/shard_map/ppermute | solution.py:667
  51.9 3.7 %all-to-all-done.1 = bf16[64,8,128]{2,1,0:T(8,128)(2,1)S(1)} async-done(((bf16[64,8,128]{2,1,0:T(8,128)(2,1)}), bf16[64,8,128]{2,1,0:T(8,128)(2,1)S(1)}, u32[]{:S(2)}, u32[]{:S(2)}) %all-to-all-start.1) | async-done | bytes 131104 | tf_op jit(solution)/shard_map/all_to_all | solution.py:662
  56.0 1.4 %collective-permute-start.7 = (bf16[512,128]{1,0:T(8,128)(2,1)S(1)}, bf16[512,128]{1,0:T(8,128)(2,1)S(1)}, u32[]{:S(2)}, u32[]{:S(2)}) collective-permute-start(bf16[512,128]{1,0:T(8,128)(2,1)S(1)} %bitcast.7), channel_id=1, source_target_pairs={{0,2},{1,3},{2,0},{3,1},{4,6},{5,7},{6,4},{7,5},{8,10},{9,11},{10,... | collective-permute-start | bytes 393224 | tf_op jit(solution)/shard_map/ppermute | solution.py:642
  57.5 1.1 collective-permute-start.6
  58.5 6.8 %analyse_own.1 = (bf16[8,4,32,1024]{3,2,1,0:T(8,128)(2,1)S(1)}, f32[32,64]{1,0:T(8,128)S(1)}, bf16[8,2,80,1024]{3,2,1,0:T(8,128)(2,1)S(1)}, bf16[8,4,32,1024]{3,2,1,0:T(8,128)(2,1)S(1)}) custom-call(s32[2]{0:T(128)S(1)} %get-tuple-element.31.where, bf16[512,128]{1,0:T(8,128)(2,1)S(1)} %bitcast.9, bf16[8,2,256,1024]{3,2,1,0:T(8,128)(2,1)} %legendre.3, ...), custom_call_target="tpu_custom_call" | custom-call | flops 500000000 | bytes 5242880 | tf_op jit(solution)/shard_map/analyse_own/pallas_call | solution.py:368
  65.4 5.5 %analyse.1 = (bf16[8,4,96,1024]{3,2,1,0:T(8,128)(2,1)S(1)}, f32[48,128]{1,0:T(8,128)S(1)}, f32[48,128]{1,0:T(8,128)S(1)}) custom-call(s32[2]{0:T(128)S(1)} %get-tuple-element.31.where, bf16[512,128]{1,0:T(8,128)(2,1)S(1)} %collective-permute-done.6.got1, bf16[512,128]{1,0:T(8,128)(2,1)S(1)} %collective-permute-done.7.got2, ...), custom_call_target="tpu_custom_call" | custom-call | flops 1500000000 | bytes 12582912 | tf_op jit(solution)/shard_map/analyse/pallas_call | solution.py:448
  70.9 2.7 %collective-permute-start.9 = (f32[48,128]{1,0:T(8,128)S(1)}, f32[48,128]{1,0:T(8,128)S(1)}, u32[]{:S(2)}, u32[]{:S(2)}) collective-permute-start(f32[48,128]{1,0:T(8,128)S(1)} %get-tuple-element.56), channel_id=1, source_target_pairs={{0,4},{4,0},{1,5},{5,1},{2,6},{6,2},{3,7},{7,3},{8,12},{12,8},{9,1... | collective-permute-start | bytes 73736 | tf_op jit(solution)/shard_map/ppermute | solution.py:626
  73.5 0.8 collective-permute-done.9
  74.4 3.1 %collective-permute-start.12 = (f32[48,128]{1,0:T(8,128)S(1)}, f32[48,128]{1,0:T(8,128)S(1)}, u32[]{:S(2)}, u32[]{:S(2)}) collective-permute-start(f32[48,128]{1,0:T(8,128)S(1)} %add.24), channel_id=1, source_target_pairs={{0,24},{8,16},{16,8},{24,0},{32,56},{40,48},{48,40},{56,32},{1,25}... | collective-permute-start | bytes 73736 | tf_op jit(solution)/shard_map/ppermute | solution.py:626
  77.5 0.5 collective-permute-start.10
  77.9 0.9 collective-permute-done.12
  78.9 2.3 %collective-permute-done.11 = f32[48,128]{1,0:T(8,128)S(1)} collective-permute-done((f32[48,128]{1,0:T(8,128)S(1)}, f32[48,128]{1,0:T(8,128)S(1)}, u32[]{:S(2)}, u32[]{:S(2)}) %collective-permute-start.11) | collective-permute-done | bytes 24608 | tf_op jit(solution)/shard_map/ppermute | solution.py:626
  81.2 3.6 %collective-permute-start.13 = (f32[48,128]{1,0:T(8,128)S(1)}, f32[48,128]{1,0:T(8,128)S(1)}, u32[]{:S(2)}, u32[]{:S(2)}) collective-permute-start(f32[48,128]{1,0:T(8,128)S(1)} %add_add_fusion.1), channel_id=1, source_target_pairs={{0,32},{8,40},{16,48},{24,56},{32,0},{40,8},{48,16},{56,24},{1,33}... | collective-permute-start | bytes 73736 | tf_op jit(solution)/shard_map/ppermute | solution.py:626
  84.7 3.1 %collective-permute-done.13 = f32[48,128]{1,0:T(8,128)S(1)} collective-permute-done((f32[48,128]{1,0:T(8,128)S(1)}, f32[48,128]{1,0:T(8,128)S(1)}, u32[]{:S(2)}, u32[]{:S(2)}) %collective-permute-start.13) | collective-permute-done | bytes 24608 | tf_op jit(solution)/shard_map/ppermute | solution.py:626
  87.8 2.5 %collective-permute-start.16 = (f32[48,128]{1,0:T(8,128)S(1)}, f32[48,128]{1,0:T(8,128)S(1)}, u32[]{:S(2)}, u32[]{:S(2)}) collective-permute-start(f32[48,128]{1,0:T(8,128)S(1)} %add.28), channel_id=1, source_target_pairs={{0,192},{64,128},{128,64},{192,0},{1,193},{65,129},{129,65},{193,1... | collective-permute-start | bytes 73736 | tf_op jit(solution)/shard_map/ppermute | solution.py:626
  90.4 0.4 collective-permute-start.15
  91.1 0.6 collective-permute-done.16
  91.7 2.8 %collective-permute-done.15 = f32[48,128]{1,0:T(8,128)S(1)} collective-permute-done((f32[48,128]{1,0:T(8,128)S(1)}, f32[48,128]{1,0:T(8,128)S(1)}, u32[]{:S(2)}, u32[]{:S(2)}) %collective-permute-start.15) | collective-permute-done | bytes 24608 | tf_op jit(solution)/shard_map/ppermute | solution.py:626
  94.6 14.2 %all_to_all.15 = f32[8,48,128]{2,1,0:T(8,128)S(1)} all-to-all(f32[8,48,128]{2,1,0:T(8,128)S(1)} %broadcast_in_dim.2), channel_id=1, replica_groups=mesh['ma_0'=4,'ma_1'=8,'ma_2'=2,'vert'=4] {'ma_2','vert'}, dimensions={0} | all-to-all | bytes 393216 | tf_op jit(solution)/shard_map/all_to_all | solution.py:674
  108.8 7.9 %factors.1 = (bf16[128,512]{1,0:T(8,128)(2,1)S(1)}, f32[128,128]{1,0:T(8,128)}) custom-call(f32[2,4,48,128]{3,2,1,0:T(8,128)S(1)} %bitcast.11), custom_call_target="tpu_custom_call" | custom-call | flops 100000000 | bytes 1048576 | tf_op jit(solution)/shard_map/factors/pallas_call | solution.py:572
  116.8 2.2 %mix.1 = bf16[32,8,4,1024]{3,2,1,0:T(4,128)(2,1)} custom-call(bf16[128,512]{1,0:T(8,128)(2,1)S(1)} %get-tuple-element.57.weights, bf16[8,4,32,1024]{3,2,1,0:T(8,128)(2,1)S(1)} %get-tuple-element.51.own, bf16[8,4,96,1024]{3,2,1,0:T(8,128)(2,1)S(1)} %get-tuple-element.58.rest), custom_call_target="tpu_custom_call" | custom-call | flops 1100000000 | bytes 10485760 | tf_op jit(solution)/shard_map/mix/pallas_call | solution.py:608
  (29 shorter events, 0.9 us)
Async XLA Ops:
  0.6 26.1 %copy-start.3 = (s32[512]{0:T(512)S(1)}, s32[512]{0:T(512)}, u32[]{:S(2)}) copy-start(s32[512]{0:T(512)} %param.8) | copy-start | bytes 6148
  7.9 37.4 %collective-permute-start = (bf16[2,32,4,1024]{3,2,1,0:T(4,128)(2,1)}, bf16[2,32,4,1024]{3,2,1,0:T(4,128)(2,1)S(1)}, u32[]{:S(2)}, u32[]{:S(2)}) collective-permute-start(bf16[2,32,4,1024]{3,2,1,0:T(4,128)(2,1)} %get-tuple-element.38), channel_id=1, source_target_pairs={{0,1},{1,2},{2,3},{3,0},{4,5},{5,6},{6,7},{7,4},{8,9},{9,10},{10,1... | collective-permute-start | bytes 1572872 | tf_op jit(solution)/shard_map/ppermute | solution.py:653
  10.0 35.3 %collective-permute-start.1 = (bf16[2,32,4,1024]{3,2,1,0:T(4,128)(2,1)}, bf16[2,32,4,1024]{3,2,1,0:T(4,128)(2,1)S(1)}, u32[]{:S(2)}, u32[]{:S(2)}) collective-permute-start(bf16[2,32,4,1024]{3,2,1,0:T(4,128)(2,1)} %get-tuple-element.39), channel_id=1, source_target_pairs={{0,2},{1,3},{2,0},{3,1},{4,6},{5,7},{6,4},{7,5},{8,10},{9,11},{10,... | collective-permute-start | bytes 1572872 | tf_op jit(solution)/shard_map/ppermute | solution.py:653
  12.4 32.9 %collective-permute-start.2 = (bf16[2,32,4,1024]{3,2,1,0:T(4,128)(2,1)}, bf16[2,32,4,1024]{3,2,1,0:T(4,128)(2,1)}, u32[]{:S(2)}, u32[]{:S(2)}) collective-permute-start(bf16[2,32,4,1024]{3,2,1,0:T(4,128)(2,1)} %get-tuple-element.40), channel_id=1, source_target_pairs={{0,3},{1,0},{2,1},{3,2},{4,7},{5,4},{6,5},{7,6},{8,11},{9,8},{10,9... | collective-permute-start | bytes 1572872 | tf_op jit(solution)/shard_map/ppermute | solution.py:653
  13.6 23.5 %all-to-all-start = ((bf16[64,8,128]{2,1,0:T(8,128)(2,1)}), bf16[64,8,128]{2,1,0:T(8,128)(2,1)S(1)}, u32[]{:S(2)}, u32[]{:S(2)}) async-start(bf16[64,8,128]{2,1,0:T(8,128)(2,1)} %get-tuple-element.32), calls=%async_computation | async-start | bytes 262144 | tf_op jit(solution)/shard_map/all_to_all | solution.py:654
  28.9 8.2 %copy-start = (s32[256]{0:T(256)S(1)}, s32[256]{0:T(256)}, u32[]{:S(2)}) copy-start(s32[256]{0:T(256)} %counts.1) | copy-start | bytes 3076
  28.9 8.2 %copy-start.1 = (s32[256]{0:T(256)S(1)}, s32[256]{0:T(256)}, u32[]{:S(2)}) copy-start(s32[256]{0:T(256)} %begins.1) | copy-start | bytes 3076
  28.9 8.2 %copy-start.2 = (f32[256]{0:T(256)S(1)}, f32[256]{0:T(256)}, u32[]{:S(2)}) copy-start(f32[256]{0:T(256)} %weights.1) | copy-start | bytes 3076
  39.6 16.1 %all-to-all-start.1 = ((bf16[64,8,128]{2,1,0:T(8,128)(2,1)}), bf16[64,8,128]{2,1,0:T(8,128)(2,1)S(1)}, u32[]{:S(2)}, u32[]{:S(2)}) async-start(bf16[64,8,128]{2,1,0:T(8,128)(2,1)} %bitcast.3), calls=%async_computation.1 | async-start | bytes 262144 | tf_op jit(solution)/shard_map/all_to_all | solution.py:662
  49.7 5.9 %collective-permute-start.3 = (f32[32,128]{1,0:T(8,128)S(1)}, f32[32,128]{1,0:T(8,128)S(1)}, u32[]{:S(2)}, u32[]{:S(2)}) collective-permute-start(f32[32,128]{1,0:T(8,128)S(1)} %get-tuple-element.42), channel_id=1, source_target_pairs={{0,3},{1,0},{2,1},{3,2},{4,7},{5,4},{6,5},{7,6},{8,11},{9,8},{10,9... | collective-permute-start | bytes 49160 | tf_op jit(solution)/shard_map/ppermute | solution.py:667
  49.8 5.8 %collective-permute-start.4 = (f32[32,128]{1,0:T(8,128)S(1)}, f32[32,128]{1,0:T(8,128)S(1)}, u32[]{:S(2)}, u32[]{:S(2)}) collective-permute-start(f32[32,128]{1,0:T(8,128)S(1)} %get-tuple-element.43), channel_id=1, source_target_pairs={{0,2},{1,3},{2,0},{3,1},{4,6},{5,7},{6,4},{7,5},{8,10},{9,11},{10,... | collective-permute-start | bytes 49160 | tf_op jit(solution)/shard_map/ppermute | solution.py:667
  51.9 3.8 %collective-permute-start.5 = (f32[32,128]{1,0:T(8,128)S(1)}, f32[32,128]{1,0:T(8,128)S(1)}, u32[]{:S(2)}, u32[]{:S(2)}) collective-permute-start(f32[32,128]{1,0:T(8,128)S(1)} %get-tuple-element.44), channel_id=1, source_target_pairs={{0,1},{1,2},{2,3},{3,0},{4,5},{5,6},{6,7},{7,4},{8,9},{9,10},{10,1... | collective-permute-start | bytes 49160 | tf_op jit(solution)/shard_map/ppermute | solution.py:667
  55.7 9.6 %collective-permute-start.8 = (bf16[512,128]{1,0:T(8,128)(2,1)S(1)}, bf16[512,128]{1,0:T(8,128)(2,1)S(1)}, u32[]{:S(2)}, u32[]{:S(2)}) collective-permute-start(bf16[512,128]{1,0:T(8,128)(2,1)S(1)} %bitcast.6), channel_id=1, source_target_pairs={{0,1},{1,2},{2,3},{3,0},{4,5},{5,6},{6,7},{7,4},{8,9},{9,10},{10,1... | collective-permute-start | bytes 393224 | tf_op jit(solution)/shard_map/ppermute | solution.py:642
  56.0 9.3 %collective-permute-start.7 = (bf16[512,128]{1,0:T(8,128)(2,1)S(1)}, bf16[512,128]{1,0:T(8,128)(2,1)S(1)}, u32[]{:S(2)}, u32[]{:S(2)}) collective-permute-start(bf16[512,128]{1,0:T(8,128)(2,1)S(1)} %bitcast.7), channel_id=1, source_target_pairs={{0,2},{1,3},{2,0},{3,1},{4,6},{5,7},{6,4},{7,5},{8,10},{9,11},{10,... | collective-permute-start | bytes 393224 | tf_op jit(solution)/shard_map/ppermute | solution.py:642
  57.5 7.9 %collective-permute-start.6 = (bf16[512,128]{1,0:T(8,128)(2,1)S(1)}, bf16[512,128]{1,0:T(8,128)(2,1)S(1)}, u32[]{:S(2)}, u32[]{:S(2)}) collective-permute-start(bf16[512,128]{1,0:T(8,128)(2,1)S(1)} %bitcast.8), channel_id=1, source_target_pairs={{0,3},{1,0},{2,1},{3,2},{4,7},{5,4},{6,5},{7,6},{8,11},{9,8},{10,9... | collective-permute-start | bytes 393224 | tf_op jit(solution)/shard_map/ppermute | solution.py:642
  70.9 3.5 %collective-permute-start.9 = (f32[48,128]{1,0:T(8,128)S(1)}, f32[48,128]{1,0:T(8,128)S(1)}, u32[]{:S(2)}, u32[]{:S(2)}) collective-permute-start(f32[48,128]{1,0:T(8,128)S(1)} %get-tuple-element.56), channel_id=1, source_target_pairs={{0,4},{4,0},{1,5},{5,1},{2,6},{6,2},{3,7},{7,3},{8,12},{12,8},{9,1... | collective-permute-start | bytes 73736 | tf_op jit(solution)/shard_map/ppermute | solution.py:626
  74.4 4.5 %collective-permute-start.12 = (f32[48,128]{1,0:T(8,128)S(1)}, f32[48,128]{1,0:T(8,128)S(1)}, u32[]{:S(2)}, u32[]{:S(2)}) collective-permute-start(f32[48,128]{1,0:T(8,128)S(1)} %add.24), channel_id=1, source_target_pairs={{0,24},{8,16},{16,8},{24,0},{32,56},{40,48},{48,40},{56,32},{1,25}... | collective-permute-start | bytes 73736 | tf_op jit(solution)/shard_map/ppermute | solution.py:626
  77.5 3.7 %collective-permute-start.11 = (f32[48,128]{1,0:T(8,128)S(1)}, f32[48,128]{1,0:T(8,128)S(1)}, u32[]{:S(2)}, u32[]{:S(2)}) collective-permute-start(f32[48,128]{1,0:T(8,128)S(1)} %add.24), channel_id=1, source_target_pairs={{0,16},{8,24},{16,0},{24,8},{32,48},{40,56},{48,32},{56,40},{1,17}... | collective-permute-start | bytes 73736 | tf_op jit(solution)/shard_map/ppermute | solution.py:626
  77.5 3.7 %collective-permute-start.10 = (f32[48,128]{1,0:T(8,128)S(1)}, f32[48,128]{1,0:T(8,128)S(1)}, u32[]{:S(2)}, u32[]{:S(2)}) collective-permute-start(f32[48,128]{1,0:T(8,128)S(1)} %add.24), channel_id=1, source_target_pairs={{0,8},{8,0},{16,24},{24,16},{32,40},{40,32},{48,56},{56,48},{1,9},... | collective-permute-start | bytes 73736 | tf_op jit(solution)/shard_map/ppermute | solution.py:626
  81.2 6.7 %collective-permute-start.13 = (f32[48,128]{1,0:T(8,128)S(1)}, f32[48,128]{1,0:T(8,128)S(1)}, u32[]{:S(2)}, u32[]{:S(2)}) collective-permute-start(f32[48,128]{1,0:T(8,128)S(1)} %add_add_fusion.1), channel_id=1, source_target_pairs={{0,32},{8,40},{16,48},{24,56},{32,0},{40,8},{48,16},{56,24},{1,33}... | collective-permute-start | bytes 73736 | tf_op jit(solution)/shard_map/ppermute | solution.py:626
  87.8 3.9 %collective-permute-start.16 = (f32[48,128]{1,0:T(8,128)S(1)}, f32[48,128]{1,0:T(8,128)S(1)}, u32[]{:S(2)}, u32[]{:S(2)}) collective-permute-start(f32[48,128]{1,0:T(8,128)S(1)} %add.28), channel_id=1, source_target_pairs={{0,192},{64,128},{128,64},{192,0},{1,193},{65,129},{129,65},{193,1... | collective-permute-start | bytes 73736 | tf_op jit(solution)/shard_map/ppermute | solution.py:626
  90.4 4.2 %collective-permute-start.15 = (f32[48,128]{1,0:T(8,128)S(1)}, f32[48,128]{1,0:T(8,128)S(1)}, u32[]{:S(2)}, u32[]{:S(2)}) collective-permute-start(f32[48,128]{1,0:T(8,128)S(1)} %add.28), channel_id=1, source_target_pairs={{0,128},{64,192},{128,0},{192,64},{1,129},{65,193},{129,1},{193,65... | collective-permute-start | bytes 73736 | tf_op jit(solution)/shard_map/ppermute | solution.py:626
  90.8 3.8 %collective-permute-start.14 = (f32[48,128]{1,0:T(8,128)S(1)}, f32[48,128]{1,0:T(8,128)S(1)}, u32[]{:S(2)}, u32[]{:S(2)}) collective-permute-start(f32[48,128]{1,0:T(8,128)S(1)} %add.28), channel_id=1, source_target_pairs={{0,64},{64,0},{128,192},{192,128},{1,65},{65,1},{129,193},{193,129... | collective-permute-start | bytes 73736 | tf_op jit(solution)/shard_map/ppermute | solution.py:626
